TPU v7x, 256 devices: a whole 4x4x8 slice. The times are simulated.
256 devices in a mesh: slab: 32 (over z, x), freq: 8 (over y, core).
Axes of the slice: x: 4, y: 4, z: 8, core: 2. Of those that a mesh axis runs over, the one named last changes fastest.
Arguments:
- wavefield: float32 [2, 96, 32, 32768], P(None, 'freq', None, 'slab'), may hold values from -6 to 6
- observed: float32 [2, 96, 32, 16384], P(None, None, 'freq', 'slab'), may hold values from -6 to 6
- filters: float32 [32, 256], P('freq'), may hold values from -0.375 to 0.375
- mute: int32 [32, 16384], P('freq', 'slab'), may hold values from 0 to 511
- send_cell: int32 [32, 1024], P('slab'), may hold values from 0 to 1023, as said below
- send_count: int32 [32, 32], P('slab'), may hold values from 0 to 32, as said below
- recv_pos: int32 [32, 1024], P('slab'), may hold values from -1 to 511, as said below
Outputs:
- adjoint: float32 [2, 96, 32, 32768], P(None, 'freq', None, 'slab')
Inputs may be any that keep to these rules, and one draw needn't show every extreme that they name: `send_cell`: row s lists distinct cells of slab s; slots at or beyond send_count[s, d] hold cells too and carry no receiver. `send_count`: for every trace group d the column d sums to 512, and its largest entry is 32. `recv_pos`: entry s * 32 + k of row d is the trace's place in group d when k < send_count[s, d], else -1; the places of one row are each of 0 to 511 once.
All inputs are finite; a program needn't handle non-finite values.
Results may differ from a plain program's by a relative error of at most 0.0003.
Values sent between devices are 32-bit elements; how exact they have to be, the bound alone decides.
No kernel may reach another device: no remote copies, remote signals or barrier semaphores. Data moves between devices by JAX's collectives and lax.ppermute only.
A program may use at most 128 MiB of HBM per device.

v0:
```python
import math

import jax
import jax.numpy as jnp
from jax import lax
from jax.sharding import PartitionSpec as P

F = 96
NT = 1024
TAPS = 256
K0 = 8


def tables():
    bins_used = K0 + jnp.arange(F, dtype=jnp.int32)
    sample_ids = jnp.arange(NT, dtype=jnp.int32)
    phases = bins_used[:, None] * sample_ids[None, :] % NT
    angles = phases.astype(jnp.float32) * (2.0 * math.pi / NT)
    cosine = jnp.cos(angles)
    sine_part = jnp.sin(angles)
    inverse = jnp.stack([cosine, -sine_part]) / math.sqrt(F)
    forward = jnp.stack([cosine, -sine_part]) / math.sqrt(NT)
    return (inverse, forward)


def shifted_rows(padded_taps):
    width = padded_taps.shape[-1]
    taps_count = width // 2
    tiled = jnp.tile(padded_taps, (1, taps_count))
    trimmed = tiled[:, : taps_count * (width - 1)]
    return trimmed.reshape(padded_taps.shape[0], taps_count, width - 1)[:, :, :taps_count]


def toeplitz_all(filters):
    zero_taps = jnp.zeros_like(filters)
    lower = shifted_rows(jnp.concatenate([filters, zero_taps], axis=1))
    upper = shifted_rows(jnp.concatenate([zero_taps, filters], axis=1))
    return (lower, upper)


def relay(values):
    return lax.all_to_all(values, "slab", split_axis=3, concat_axis=3, tiled=True)


def residual_spectra(spectra, observed, filters, mute):
    inverse, forward = tables()
    lower, upper = toeplitz_all(filters)
    traces = jnp.einsum("cfst,cfn->stn", spectra, inverse, precision=lax.Precision.HIGHEST)
    shaped = traces.reshape(traces.shape[:2] + (NT // TAPS, TAPS))
    earlier = jnp.concatenate([jnp.zeros_like(shaped[:, :, :1, :]), shaped[:, :, :-1, :]], axis=2)
    filtered = jnp.einsum("stbi,sij->stbj", shaped, lower, precision=lax.Precision.HIGHEST)
    filtered = filtered + jnp.einsum(
        "stbi,sij->stbj", earlier, upper, precision=lax.Precision.HIGHEST
    )
    filtered = filtered.reshape(traces.shape)
    keeper = jnp.arange(NT, dtype=jnp.int32)[None, None, :] >= mute[:, :, None]
    filtered = jnp.where(keeper, filtered, 0.0)
    return (
        jnp.einsum("stn,cfn->cfst", filtered, forward, precision=lax.Precision.HIGHEST) - observed
    )


def on_device(wavefield, observed, filters, mute, send_cell, send_count, recv_pos):
    cells_here = send_cell[0]
    cell_count = wavefield.shape[3]
    picker = (jnp.arange(cell_count, dtype=jnp.int32)[:, None] == cells_here[None, :]).astype(
        jnp.float32
    )
    samples = jnp.einsum("cfnk,ks->cfns", wavefield, picker, precision=lax.Precision.HIGHEST)
    arrived = relay(samples)
    positions = recv_pos[0]
    group_traces = observed.shape[3]
    placer = (positions[:, None] == jnp.arange(group_traces, dtype=jnp.int32)[None, :]).astype(
        jnp.float32
    )
    compact = jnp.einsum("cfns,sr->cfnr", arrived, placer, precision=lax.Precision.HIGHEST)
    spectra = lax.all_to_all(compact, "freq", split_axis=2, concat_axis=1, tiled=True)
    residual = residual_spectra(spectra, observed, filters, mute)
    returning = lax.all_to_all(residual, "freq", split_axis=1, concat_axis=2, tiled=True)
    picked = jnp.einsum("cfnr,sr->cfns", returning, placer, precision=lax.Precision.HIGHEST)
    returned = relay(picked)
    slab_count = lax.axis_size("slab")
    slot_rows = cells_here.shape[0] // slab_count
    living = (jnp.arange(slot_rows, dtype=jnp.int32)[None, :] < send_count[0][:, None]).reshape(-1)
    kept = jnp.where(living, returned, 0.0)
    return jnp.einsum("cfns,ks->cfnk", kept, picker, precision=lax.Precision.HIGHEST)


def solution(mesh):
    return jax.shard_map(
        on_device,
        mesh=mesh,
        in_specs=(
            P(None, "freq", None, "slab"),
            P(None, None, "freq", "slab"),
            P("freq", None),
            P("freq", "slab"),
            P("slab", None),
            P("slab", None),
            P("slab", None),
        ),
        out_specs=P(None, "freq", None, "slab"),
        check_vma=False,
    )
```

profile of v0, /device:TPU:1, one launch (start us, length us, event | category | flops | bytes accessed | tf_op | source)
XLA Modules:
  0.0 463.6 jit_solution(10230397493511835162)
XLA Ops:
  0.0 0.0 copy-start
  0.0 1.9 copy-done
  1.9 7.6 %fusion.24 = f32[2,12,32,1024]{3,2,1,0:T(8,128)} fusion(f32[2,12,32,1024]{3,2,1,0:T(8,128)S(1)} %copy-done, s32[1024]{0:T(1024)} %bitcast.88), kind=kOutput, calls=%fused_computation.23 | convolution fusion | flops 9664724992 | bytes 6295552 | tf_op jit(solution)/shard_map/cfnk,ks->cfns/dot_general | solution.py:69
  9.5 17.2 %copy.36 = f32[2,12,32,1024]{2,0,1,3:T(2,128)} copy(f32[2,12,32,1024]{3,2,1,0:T(8,128)} %fusion.24) | data formatting | bytes 6291456 | tf_op jit(solution)/shard_map/cfnk,ks->cfns/dot_general | solution.py:69
  26.7 14.6 %reshape.142 = f32[32,1,24576]{2,1,0:T(1,128)} reshape(f32[1024,12,2,32]{3,2,1,0:T(2,128)} %bitcast.77) | data formatting | bytes 6291456
  41.3 83.3 %all_to_all.46 = f32[32,1,24576]{2,1,0:T(1,128)S(1)} all-to-all(f32[32,1,24576]{2,1,0:T(1,128)} %reshape.142), channel_id=1, replica_groups=mesh['slab'=32,'freq'=8] {'slab'}, dimensions={0} | all-to-all | bytes 6291456 | tf_op jit(solution)/shard_map/all_to_all | solution.py:42
  124.5 0.5 broadcast.130
  125.0 10.8 %reduce = f32[32,24576]{1,0:T(8,128)} reduce(f32[32,1,24576]{2,1,0:T(1,128)S(1)} %all_to_all.46, f32[]{:T(128)} %broadcast.130), dimensions={1}, to_apply=%all_to_all.32.reduce_sub_computation | reduce | bytes 6291460 | tf_op jit(solution)/shard_map/all_to_all | solution.py:42
  135.8 0.0 copy-start.6
  135.8 13.3 %reshape.143 = f32[1024,12,2,32]{3,2,1,0:T(2,128)} reshape(f32[32,24576]{1,0:T(8,128)} %reduce) | data formatting | bytes 6291456
  149.2 0.0 copy-done.6
  149.2 27.0 %fusion.2 = f32[2,12,32,512]{3,2,1,0:T(8,128)S(1)} fusion(f32[2,12,32,1024]{2,0,1,3:T(2,128)} %bitcast.78, s32[1024]{0:T(1024)S(1)} %bitcast.86), kind=kOutput, calls=%fused_computation.2 | convolution fusion | flops 4832362496 | bytes 4722688 | tf_op jit(solution)/shard_map/cfns,sr->cfnr/dot_general | solution.py:76
  176.2 0.0 copy-start.9
  176.2 2.4 copy.38
  178.6 7.3 %all-to-all-start.1 = ((f32[2,12,32,512]{3,0,1,2:T(2,128)}), f32[2,12,32,512]{3,0,1,2:T(2,128)}, u32[]{:S(2)}, u32[]{:S(2)}) async-start(f32[2,12,32,512]{3,0,1,2:T(2,128)} %copy.38), calls=%async_computation.1 | async-start | bytes 3145728 | tf_op jit(solution)/shard_map/all_to_all | solution.py:77
  185.8 0.0 copy-done.9
  185.9 0.4 broadcast_bitcast_fusion
  186.2 1.4 copy.65
  187.6 1.5 slice.20
  189.1 5.1 %reshape.130 = f32[4,256,511]{2,1,0:T(8,128)} reshape(f32[4,130816]{1,0:T(4,128)} %slice.20) | data formatting | bytes 4186112 | tf_op jit(solution)/shard_map/reshape | solution.py:31
  194.2 1.4 copy.66
  195.5 0.1 slice.23
  195.7 3.6 reshape.131
  199.3 1.6 fusion.45
  200.9 0.0 copy-start.4
  200.9 0.1 fusion.37
  201.0 5.7 %all-to-all-done.1 = f32[2,12,32,512]{3,0,1,2:T(2,128)} async-done(((f32[2,12,32,512]{3,0,1,2:T(2,128)}), f32[2,12,32,512]{3,0,1,2:T(2,128)}, u32[]{:S(2)}, u32[]{:S(2)}) %all-to-all-start.1) | async-done | bytes 1572896 | tf_op jit(solution)/shard_map/all_to_all | solution.py:77
  206.7 0.0 copy-done.4
  206.7 2.4 copy.39
  209.1 0.0 copy-start.3
  209.1 7.5 %convolution_bitcast_fusion = f32[4,512,4,256]{3,1,2,0:T(8,128)S(1)} fusion(f32[2,96,4,512,1]{3,2,1,0,4:T(4,128)S(1)} %bitcast.84, f32[2,12,4,8,256]{4,3,2,1,0:T(8,128)S(1)} %bitcast.85), kind=kOutput, calls=%fused_computation.17 | convolution fusion | flops 4831838208 | bytes 10747904 | tf_op jit(solution)/shard_map/cfst,cfn->stn/dot_general | solution.py:48
  216.6 0.0 copy-done.3
  216.6 0.0 copy-start.2
  216.6 8.3 %fusion.31 = f32[4,512,4,256]{1,3,2,0:T(8,128)S(1)} fusion(f32[4,512,4,256]{3,1,2,0:T(8,128)S(1)} %convolution_bitcast_fusion, f32[4,256,511]{2,1,0:T(8,128)S(1)} %copy-done.3), kind=kOutput, calls=%fused_computation.29 | convolution fusion | flops 6442450944 | bytes 17825792 | tf_op jit(solution)/shard_map/stbi,sij->stbj/dot_general | solution.py:51
  224.9 0.0 copy-done.2
  224.9 9.3 %fusion.15 = f32[4,512,4,256]{1,3,2,0:T(8,128)} fusion(f32[4,512,4,256]{1,3,2,0:T(8,128)S(1)} %fusion.31, f32[4,512,4,256]{3,1,2,0:T(8,128)S(1)} %convolution_bitcast_fusion, f32[4,256,511]{2,1,0:T(8,128)S(1)} %copy-done.2), kind=kOutput, calls=%fused_computation.16 | convolution fusion | flops 4833935360 | bytes 24117248 | tf_op jit(solution)/shard_map/stbi,sij->stbj/dot_general | solution.py:52
  234.2 0.0 copy-start.5
  234.2 0.0 copy-start.7
  234.3 8.8 %copy.44 = f32[4,512,1024]{2,1,0:T(8,128)} copy(f32[4,512,1024]{1,2,0:T(8,128)} %bitcast.76) | data formatting | bytes 16777216 | tf_op jit(solution)/shard_map/reshape | solution.py:55
  243.0 0.0 copy-done.5
  243.0 0.0 copy-done.7
  243.0 11.1 %copy_subtract_fusion = f32[2,96,4,512]{3,1,2,0:T(8,128)S(1)} fusion(f32[2,96,4,512]{3,2,1,0:T(4,128)} %param.8, f32[4,512,1024]{2,1,0:T(8,128)} %copy.44, s32[4,512]{1,0:T(4,128)S(1)} %copy-done.7, f32[1,96,1024]{2,1,0:T(8,128)S(1)} %copy-done.5, f32[1,96,1024]{2,1,0:T(8,128)S(1)} %get-tuple-element.7), kind=kOutput, calls=%fused_computation.26 | convolution fusion | flops 4836818944 | bytes 12328960 | tf_op jit(solution)/shard_map/stn,cfn->cfst/dot_general | solution.py:59
  254.1 1.0 copy.46
  255.2 24.1 %all_to_all.47 = f32[2,96,4,512]{3,2,0,1:T(4,128)S(1)} all-to-all(f32[2,96,4,512]{3,2,0,1:T(4,128)S(1)} %copy.46), channel_id=1, replica_groups=mesh['slab'=32,'freq'=8] {'freq'}, dimensions={1} | all-to-all | bytes 3145728 | tf_op jit(solution)/shard_map/all_to_all | solution.py:79
  279.2 0.8 copy.48
  280.1 2.9 fusion.21
  283.0 13.2 %copy.50 = f32[2,12,32,1024]{2,0,1,3:T(2,128)} copy(f32[2,12,32,1024]{3,2,1,0:T(8,128)S(1)} %fusion.21) | data formatting | bytes 6291456 | tf_op jit(solution)/shard_map/cfnr,sr->cfns/dot_general | solution.py:80
  296.2 14.6 %reshape.144 = f32[32,1,24576]{2,1,0:T(1,128)} reshape(f32[1024,12,2,32]{3,2,1,0:T(2,128)} %bitcast.79) | data formatting | bytes 6291456
  310.9 0.0 copy-start.10
  310.9 5.8 %all-to-all-start.3 = ((f32[32,1,24576]{2,1,0:T(1,128)}), f32[32,1,24576]{2,1,0:T(1,128)S(1)}, u32[]{:S(2)}, u32[]{:S(2)}) async-start(f32[32,1,24576]{2,1,0:T(1,128)} %reshape.144), calls=%async_computation.3 | async-start | bytes 6291456 | tf_op jit(solution)/shard_map/all_to_all | solution.py:42
  316.7 0.0 copy-done.10
  316.7 0.1 iota_compare_fusion.4
  316.8 0.1 lt.31
  316.8 70.4 %all-to-all-done.3 = f32[32,1,24576]{2,1,0:T(1,128)S(1)} async-done(((f32[32,1,24576]{2,1,0:T(1,128)}), f32[32,1,24576]{2,1,0:T(1,128)S(1)}, u32[]{:S(2)}, u32[]{:S(2)}) %all-to-all-start.3) | async-done | bytes 3145760 | tf_op jit(solution)/shard_map/all_to_all | solution.py:42
  387.3 10.8 %reduce.1 = f32[32,24576]{1,0:T(8,128)} reduce(f32[32,1,24576]{2,1,0:T(1,128)S(1)} %all-to-all-done.3, f32[]{:T(128)} %broadcast.130), dimensions={1}, to_apply=%all_to_all.41.reduce_sub_computation | reduce | bytes 6291460 | tf_op jit(solution)/shard_map/all_to_all | solution.py:42
  398.1 13.3 %reshape.145 = f32[1024,12,2,32]{3,2,1,0:T(2,128)} reshape(f32[32,24576]{1,0:T(8,128)} %reduce.1) | data formatting | bytes 6291456
  411.4 0.0 copy-start.8
  411.4 9.7 %broadcast_select_fusion = f32[2,12,32,1024]{2,0,1,3:T(2,128)S(1)} fusion(pred[1024]{0:T(1024)(128)(4,1)S(1)} %lt.31, f32[1024,12,2,32]{3,2,1,0:T(2,128)} %reshape.145), kind=kLoop, calls=%fused_computation.4 | loop fusion | flops 786432 | bytes 6292480 | tf_op jit(solution)/shard_map/jit(_where)/select_n | solution.py:85
  421.1 0.0 copy-done.8
  421.1 0.0 copy-start.1
  421.2 42.0 %fusion = f32[2,12,32,1024]{3,2,1,0:T(8,128)} fusion(f32[2,12,32,1024]{2,0,1,3:T(2,128)S(1)} %broadcast_select_fusion, s32[1024]{0:T(1024)S(1)} %bitcast.89), kind=kOutput, calls=%fused_computation | convolution fusion | flops 9664724992 | bytes 6295552 | tf_op jit(solution)/shard_map/cfns,ks->cfnk/dot_general | solution.py:86
  463.2 0.0 copy-done.1
  (2 shorter events, 0.0 us)
Async XLA Ops:
  0.0 1.9 copy-start
  135.8 13.3 %copy-start.6 = (s32[1,1024]{1,0:T(1,128)S(1)}, s32[1,1024]{1,0:T(1,128)}, u32[]{:S(2)}) copy-start(s32[1,1024]{1,0:T(1,128)} %param.13) | copy-start | bytes 12292
  176.2 9.7 %copy-start.9 = (f32[4,256]{1,0:T(4,128)S(1)}, f32[4,256]{1,0:T(4,128)}, u32[]{:S(2)}) copy-start(f32[4,256]{1,0:T(4,128)} %param.9) | copy-start | bytes 12292
  178.6 28.1 %all-to-all-start.1 = ((f32[2,12,32,512]{3,0,1,2:T(2,128)}), f32[2,12,32,512]{3,0,1,2:T(2,128)}, u32[]{:S(2)}, u32[]{:S(2)}) async-start(f32[2,12,32,512]{3,0,1,2:T(2,128)} %copy.38), calls=%async_computation.1 | async-start | bytes 3145728 | tf_op jit(solution)/shard_map/all_to_all | solution.py:77
  200.9 5.8 %copy-start.4 = (f32[1,96,1024]{2,1,0:T(8,128)}, f32[1,96,1024]{2,1,0:T(8,128)S(1)}, u32[]{:S(2)}) copy-start(f32[1,96,1024]{2,1,0:T(8,128)S(1)} %get-tuple-element.8) | copy-start | bytes 1179652
  209.1 7.5 %copy-start.3 = (f32[4,256,511]{2,1,0:T(8,128)S(1)}, f32[4,256,511]{2,1,0:T(8,128)}, u32[]{:S(2)}) copy-start(f32[4,256,511]{2,1,0:T(8,128)} %reshape.130) | copy-start | bytes 6279172
  216.6 8.3 %copy-start.2 = (f32[4,256,511]{2,1,0:T(8,128)S(1)}, f32[4,256,511]{2,1,0:T(8,128)}, u32[]{:S(2)}) copy-start(f32[4,256,511]{2,1,0:T(8,128)} %reshape.131) | copy-start | bytes 6279172
  234.2 8.8 %copy-start.5 = (f32[1,96,1024]{2,1,0:T(8,128)S(1)}, f32[1,96,1024]{2,1,0:T(8,128)}, u32[]{:S(2)}) copy-start(f32[1,96,1024]{2,1,0:T(8,128)} %copy-done.4) | copy-start | bytes 1179652
  234.2 8.8 %copy-start.7 = (s32[4,512]{1,0:T(4,128)S(1)}, s32[4,512]{1,0:T(4,128)}, u32[]{:S(2)}) copy-start(s32[4,512]{1,0:T(4,128)} %param.10) | copy-start | bytes 24580
  310.9 5.8 %copy-start.10 = (s32[1,32]{1,0:T(1,128)S(1)}, s32[1,32]{1,0:T(1,128)}, u32[]{:S(2)}) copy-start(s32[1,32]{1,0:T(1,128)} %param.12) | copy-start | bytes 388
  310.9 76.4 %all-to-all-start.3 = ((f32[32,1,24576]{2,1,0:T(1,128)}), f32[32,1,24576]{2,1,0:T(1,128)S(1)}, u32[]{:S(2)}, u32[]{:S(2)}) async-start(f32[32,1,24576]{2,1,0:T(1,128)} %reshape.144), calls=%async_computation.3 | async-start | bytes 6291456 | tf_op jit(solution)/shard_map/all_to_all | solution.py:42
  411.4 9.7 %copy-start.8 = (s32[1,1024]{1,0:T(1,128)S(1)}, s32[1,1024]{1,0:T(1,128)}, u32[]{:S(2)}) copy-start(s32[1,1024]{1,0:T(1,128)} %param.11) | copy-start | bytes 12292
  421.1 42.0 %copy-start.1 = (f32[2,12,32,1024]{3,2,1,0:T(8,128)S(1)}, f32[2,12,32,1024]{3,2,1,0:T(8,128)}, u32[]{:S(2)}) copy-start(f32[2,12,32,1024]{3,2,1,0:T(8,128)} %param.7) | copy-start | bytes 9437188
where the time goes:
time: 471 us; the launch traced here: 464 us
  local copies, waits for them, and re-layouts  118 us (25%)
  matrix products  116 us (25%)
  blocking collectives  107 us (23%)
  waiting for transfers between devices  76.1 us (16%)
  other arithmetic  33.1 us (7%)
  starting transfers between devices  13.1 us (3%)
    all_to_all x1, blocking collectives, relay(): lax.all_to_all(values, 'slab', split_axis=3, concat_axis=3, tiled=True)  83.3 us
    all_to_all x1, waiting for transfers between devices, relay(): lax.all_to_all(values, 'slab', split_axis=3, concat_axis=3, tiled=True)  70.4 us
    unnamed x29, local copies, waits for them, and re-layouts  61 us
    dot_general x1, matrix products, on_device(): jnp.einsum('cfns,ks->cfnk', kept, picker, precision=lax.Precision.HIGHEST)  42 us
    dot_general x1, matrix products, on_device(): jnp.einsum('cfns,sr->cfnr', arrived, placer, precision=lax.Precision.HIGH...  27 us
    all_to_all x1, blocking collectives, on_device(): lax.all_to_all(residual, 'freq', split_axis=1, concat_axis=2, tiled=True)  24.1 us
    all_to_all x2, other arithmetic, relay(): lax.all_to_all(values, 'slab', split_axis=3, concat_axis=3, tiled=True)  21.6 us
    dot_general x1, local copies, waits for them, and re-layouts, on_device(): jnp.einsum('cfnk,ks->cfns', wavefield, picker, precision=lax.Precision.HI...  17.2 us
  transfers between devices with their start and end apart: 2, of which 2 were waited for; matrix products, arithmetic and copies ran while one was open for 3% of the time, Pallas kernels for 0%

commit v1 on v0

v1 whole, which is shorter than its diff:
```python
import functools
import math

import jax
import jax.numpy as jnp
from jax import lax
from jax.experimental import pallas as pl
from jax.experimental.pallas import tpu as pltpu
from jax.sharding import PartitionSpec as P

F = 96
NT = 1024
TAPS = 256
K0 = 8
HALF = 512
NF = 8
FB = F // NF
ROWS = 2 * FB
CF = 2 * F
SLABS = 32
SLOT = 32
NSH = 4
VMEM = 60 << 20
BF = jnp.bfloat16
F32 = jnp.float32


def split(x):
    hi = x.astype(BF)
    return hi, (x - hi.astype(F32)).astype(BF)


def mm(a, b):
    return jnp.dot(a, b, preferred_element_type=F32)


def call(kernel, outs, n_in, *, smem=(), scratch=(), flops=0, nbytes=0):
    specs = [
        pl.BlockSpec(memory_space=pltpu.SMEM if i in smem else pltpu.VMEM) for i in range(n_in)
    ]
    vm = pl.BlockSpec(memory_space=pltpu.VMEM)
    return pl.pallas_call(
        kernel,
        out_shape=outs,
        in_specs=specs,
        out_specs=[vm] * len(outs),
        scratch_shapes=list(scratch),
        compiler_params=pltpu.CompilerParams(vmem_limit_bytes=VMEM),
        cost_estimate=pl.CostEstimate(flops=flops, bytes_accessed=nbytes, transcendentals=0),
    )


def sds(*shape, dtype=F32):
    return jax.ShapeDtypeStruct(shape, dtype)


def tables():
    row = jnp.arange(CF, dtype=jnp.int32)
    part = (row % ROWS) // FB
    freq = K0 + (row // ROWS) * FB + row % FB
    t = jnp.arange(NT, dtype=jnp.int32)

    def wave(f, c, t):
        angle = (f * t % NT).astype(F32) * (2.0 * math.pi / NT)
        return jnp.where(c == 0, jnp.cos(angle), -jnp.sin(angle))

    forward = wave(freq[:, None], part[:, None], t[None, :]) / math.sqrt(NT)
    inverse_t = wave(freq[None, :], part[None, :], t[:, None]) / math.sqrt(F)
    return forward, inverse_t


def operator_kernel(taps_ref, fwd_ref, inv_ref, gh_ref, gl_ref, bh_ref, bl_ref, g_ref):
    late = fwd_ref[:, HALF:]
    for n in range(NSH):
        rows = jnp.broadcast_to(taps_ref[n : n + 1, :], (TAPS, 2 * TAPS))
        band = pltpu.roll(rows, 1, 1, stride=1, stride_axis=0)
        for b in range(NT // TAPS):
            if b == 0:
                g = jnp.dot(band[:, TAPS:], inv_ref[:TAPS, :], precision=lax.Precision.HIGHEST)
            else:
                g = jnp.dot(
                    band,
                    inv_ref[(b - 1) * TAPS : (b + 1) * TAPS, :],
                    precision=lax.Precision.HIGHEST,
                )
            if b < 2:
                hi, lo = split(g)
                gh_ref[n, b * TAPS : (b + 1) * TAPS, :] = hi
                gl_ref[n, b * TAPS : (b + 1) * TAPS, :] = lo
            else:
                g_ref[(b - 2) * TAPS : (b - 1) * TAPS, :] = g
        hi, lo = split(jnp.dot(late, g_ref[...], precision=lax.Precision.HIGHEST))
        bh_ref[n] = hi
        bl_ref[n] = lo


def pack_kernel(obs_ref, pos_ref, mute_ref, out_ref, ms_ref, y_ref):
    group = obs_ref.shape[2]
    slots = pos_ref.shape[1]
    pick = (
        lax.broadcasted_iota(jnp.int32, (group, slots), 0) == jnp.broadcast_to(pos_ref[...], (group, slots))
    ).astype(F32).astype(BF)
    mh, ml = split(mute_ref[...].astype(F32))
    ms_ref[...] = mm(mh, pick) + mm(ml, pick)
    for n in range(NSH):
        hi, lo = split(obs_ref[n])
        y_ref[n] = mm(hi, pick) + mm(lo, pick)
    lane = lax.broadcasted_iota(jnp.int32, (CF, 128), 1) // SLOT
    for tile in range(SLABS // 4):
        parts = [y_ref[n, :, tile * 128 : (tile + 1) * 128] for n in range(NSH)]
        for b in range(4):
            acc = None
            for n in range(NSH):
                shift = ((n - b) % 4) * SLOT
                v = pltpu.roll(parts[n], shift, 1) if shift else parts[n]
                acc = v if acc is None else jnp.where(lane == n, v, acc)
            out_ref[4 * tile + b] = acc.reshape(NF, ROWS, 128)


def route_kernel(me_ref, x_ref, *refs):
    outs, st_ref = refs[:NF], refs[NF]
    for o in range(4):
        st_ref[8 * o : 8 * o + 8] = jnp.swapaxes(x_ref[:, 8 * o : 8 * o + 8, :], 0, 1)
    me = me_ref[0]
    for k in range(NF):
        j = lax.rem(me + k, NF)
        outs[k][...] = st_ref[pl.ds(j * NSH, NSH)]


def place_kernel(cell_ref, ms_ref, hot_ref, mc_ref):
    slots = cell_ref.shape[0]
    cells = hot_ref.shape[1]
    hot = (
        lax.broadcasted_iota(jnp.int32, (slots, cells), 1) == jnp.broadcast_to(cell_ref[...], (slots, cells))
    ).astype(F32).astype(BF)
    hot_ref[...] = hot
    hi, lo = split(ms_ref[...])
    mc_ref[...] = mm(hi, hot) + mm(lo, hot)


def trace_kernel(me_ref, *refs):
    xs = refs[:NF]
    gh_ref, gl_ref, bh_ref, bl_ref, fwd_ref, mc_ref = refs[NF : NF + 6]
    outs = refs[NF + 6 : 2 * NF + 6]
    fh_ref, fl_ref, x_ref, r_ref = refs[2 * NF + 6 :]
    me = me_ref[0]
    fh, fl = split(fwd_ref[:, :HALF])
    fh_ref[...] = fh
    fl_ref[...] = fl
    cells = x_ref.shape[1]
    width = 256
    t = lax.broadcasted_iota(jnp.int32, (HALF, width), 0).astype(F32)

    @pl.loop(0, NSH)
    def _(n):
        for k in range(NF):
            j = lax.rem(me - k + NF, NF)
            x_ref[pl.ds(pl.multiple_of(j * ROWS, 8), ROWS), :] = xs[k][n]
        for w in range(cells // width):
            at = slice(w * width, (w + 1) * width)
            live = mc_ref[NSH : NSH + 1, at]
            x = jnp.where(live > 0.5, x_ref[:, at], 0.0)
            xh, xl = split(x)
            gh = gh_ref[n]
            y = mm(gh, xh) + mm(gh, xl) + mm(gl_ref[n], xh)
            cut = mc_ref[pl.ds(n, 1), at]
            y = jnp.where(t >= cut, y, 0.0)
            yh, yl = split(y)
            bh = bh_ref[n]
            r = mm(fh_ref[...], yh) + mm(fh_ref[...], yl) + mm(fl_ref[...], yh)
            r = r + mm(bh, xh) + mm(bh, xl) + mm(bl_ref[n], xh)
            r_ref[:, at] = r
        for k in range(NF):
            j = lax.rem(me + k, NF)
            outs[k][n] = r_ref[pl.ds(pl.multiple_of(j * ROWS, 8), ROWS), :]


def finish_kernel(me_ref, z_ref, hot_ref, *refs):
    rs = refs[:NF]
    out_ref = refs[NF]
    a_ref, p_ref, s_ref = refs[NF + 1 :]
    me = me_ref[0]
    lane = lax.broadcasted_iota(jnp.int32, (NF, ROWS, 128), 2) // SLOT
    for n in range(NSH):
        for tile in range(SLABS // 4):
            acc = None
            for e in range(4):
                shift = ((e - n) % 4) * SLOT
                v = z_ref[4 * tile + e]
                if shift:
                    v = pltpu.roll(v, shift, 2)
                acc = v if acc is None else jnp.where(lane == e, v, acc)
            a_ref[:, tile * 128 : (tile + 1) * 128] = acc.reshape(CF, 128)
        hi, lo = split(a_ref[...])
        p_ref[...] = mm(hi, hot_ref[...]) + mm(lo, hot_ref[...])
        for k in range(NF):
            j = lax.rem(me - k + NF, NF)
            s_ref[j * NSH + n] = rs[k][n] - p_ref[pl.ds(pl.multiple_of(j * ROWS, 8), ROWS), :]
    for o in range(4):
        out_ref[:, 8 * o : 8 * o + 8, :] = jnp.swapaxes(s_ref[8 * o : 8 * o + 8], 0, 1)


def shift_by(values, k):
    return lax.ppermute(values, "freq", [(i, (i + k) % NF) for i in range(NF)])


def on_device(wavefield, observed, filters, mute, send_cell, send_count, recv_pos):
    cells = wavefield.shape[3]
    group = observed.shape[3]
    slots = send_cell.shape[1]
    slab = lax.axis_index("slab")
    me = lax.axis_index("freq").astype(jnp.int32).reshape(1)

    obs = observed.reshape(2, NF, FB, NSH, group).transpose(3, 1, 0, 2, 4).reshape(NSH, CF, group)
    packed, mute_slots = call(
        pack_kernel,
        [sds(SLABS, NF, ROWS, 128), sds(NSH, slots)],
        3,
        scratch=[pltpu.VMEM((NSH, CF, slots), F32)],
        flops=2 * 2 * NSH * CF * group * slots,
        nbytes=4 * NSH * CF * (group + slots),
    )(obs, recv_pos, mute)
    packed = packed.reshape(SLABS * NF, ROWS, 128)
    arrived = lax.all_to_all(packed, ("slab", "freq"), split_axis=0, concat_axis=0, tiled=True)
    arrived = arrived.reshape(SLABS, NF, ROWS, 128)
    mute_all = lax.all_gather(mute_slots, "slab")

    blocks = call(
        route_kernel,
        [sds(NSH, ROWS, cells)] * NF,
        2,
        smem=(0,),
        scratch=[pltpu.VMEM((NSH * NF, ROWS, cells), F32)],
        nbytes=8 * NSH * CF * cells,
    )(me, wavefield.reshape(ROWS, NSH * NF, cells))
    spectra = [blocks[0]] + [shift_by(blocks[k], k) for k in range(1, NF)]

    forward, inverse_t = tables()
    taps = jnp.concatenate([filters[:, ::-1], jnp.zeros_like(filters)], axis=1)
    gh, gl, bh, bl = call(
        operator_kernel,
        [sds(NSH, HALF, CF, dtype=BF)] * 2 + [sds(NSH, CF, CF, dtype=BF)] * 2,
        3,
        scratch=[pltpu.VMEM((HALF, CF), F32)],
        flops=6 * 2 * NSH * CF * (1024 * 512 + CF * HALF),
        nbytes=1 << 22,
    )(taps, forward, inverse_t)

    live = jnp.arange(SLOT, dtype=jnp.int32)[None, :] < send_count[0][:, None]
    target = jnp.where(live.reshape(-1), send_cell[0], -1).reshape(slots, 1)
    mine = lax.dynamic_slice(mute_all, (0, 0, slab * SLOT), (SLABS, NSH, SLOT))
    mine = mine.transpose(1, 0, 2).reshape(NSH, slots)
    mine = jnp.concatenate([mine, jnp.ones((NSH, slots), F32)], axis=0)
    hot, at_cells = call(
        place_kernel,
        [sds(slots, cells, dtype=BF), sds(2 * NSH, cells)],
        2,
        flops=4 * 8 * slots * cells,
        nbytes=2 * slots * cells,
    )(target, mine)

    results = call(
        trace_kernel,
        [sds(NSH, ROWS, cells)] * NF,
        NF + 7,
        smem=(0,),
        scratch=[
            pltpu.VMEM((CF, HALF), BF),
            pltpu.VMEM((CF, HALF), BF),
            pltpu.VMEM((CF, cells), F32),
            pltpu.VMEM((CF, cells), F32),
        ],
        flops=6 * NSH * cells * (2 * CF * HALF + CF * CF),
        nbytes=8 * NSH * CF * cells,
    )(me, *spectra, gh, gl, bh, bl, forward, at_cells)
    returned = [results[0]] + [shift_by(results[k], k) for k in range(1, NF)]

    (out,) = call(
        finish_kernel,
        [sds(ROWS, NSH * NF, cells)],
        NF + 3,
        smem=(0,),
        scratch=[
            pltpu.VMEM((CF, slots), F32),
            pltpu.VMEM((CF, cells), F32),
            pltpu.VMEM((NSH * NF, ROWS, cells), F32),
        ],
        flops=4 * NSH * CF * slots * cells,
        nbytes=12 * NSH * CF * cells,
    )(me, arrived, hot, *returned)
    return out.reshape(2, FB, NSH * NF, cells)


def solution(mesh):
    return jax.shard_map(
        on_device,
        mesh=mesh,
        in_specs=(
            P(None, "freq", None, "slab"),
            P(None, None, "freq", "slab"),
            P("freq", None),
            P("freq", "slab"),
            P("slab", None),
            P("slab", None),
            P("slab", None),
        ),
        out_specs=P(None, "freq", None, "slab"),
        check_vma=False,
    )
```

time: 471 us -> 238 us (0.51); the launches traced: 464 us -> 237 us
  matrix products: 116 us -> 0 us
  local copies, waits for them, and re-layouts: 118 us -> 10 us
  Pallas kernels: 0 us -> 50.4 us
  waiting for transfers between devices: 76.1 us -> 29.8 us
  starting transfers between devices: 13.1 us -> 47.5 us
  other arithmetic: 33.1 us -> 11.5 us
  blocking collectives: 107 us -> 87.1 us
    dot_general x8 -> x0, matrix products: 116 us -> none  [the longest x1 42 us: on_device(): jnp.einsum('cfns,ks->cfnk', kept, picker, precision=lax.Precision.HIGHEST)]
    all_to_all x2 -> x0, blocking collectives: 107 us -> none  [the longest x1 83.3 us: relay(): lax.all_to_all(values, 'slab', split_axis=3, concat_axis=3, tiled=True)]
    all_gather x0 -> x1, blocking collectives: none -> 87.1 us  [on_device(): mute_all = lax.all_gather(mute_slots, 'slab')]
    all_to_all x2 -> x1, waiting for transfers between devices: 76.1 us -> 0.01 us  [on_device(): lax.all_to_all(packed, ('slab', 'freq'), split_axis=0, concat_axis=0, til...]
    unnamed x29 -> x26, local copies, waits for them, and re-layouts: 61 us -> 3.39 us
    pallas_call x0 -> x6, Pallas kernels: none -> 50.4 us  [the longest x1 15.7 us: on_device(): call(trace_kernel, [sds(NSH, ROWS, cells)] * NF, NF + 7, smem=(0,), scrat...]
    dot_general x3 -> x0, local copies, waits for them, and re-layouts: 32.8 us -> none  [the longest x1 17.2 us: on_device(): jnp.einsum('cfnk,ks->cfns', wavefield, picker, precision=lax.Precision.HI...]
    ppermute x0 -> x14, starting transfers between devices: none -> 31.9 us  [shift_by(): return lax.ppermute(values, 'freq', [(i, (i + k) % NF) for i in range(NF)])]
  transfers between devices with their start and end apart: 2 -> 15, of which waited for: 2 -> 4; matrix products, arithmetic and copies ran while one was open for 3% -> 6% of each run, Pallas kernels for 0% -> 14%
where the time goes in v1:
time: 238 us; the launch traced here: 237 us
  blocking collectives  87.1 us (37%)
  Pallas kernels  50.4 us (21%)
  starting transfers between devices  47.5 us (20%)
  waiting for transfers between devices  29.8 us (13%)
  other arithmetic  11.5 us (5%)
  local copies, waits for them, and re-layouts  10 us (4%)
    all_gather x1, blocking collectives, on_device(): mute_all = lax.all_gather(mute_slots, 'slab')  87.1 us
    ppermute x14, starting transfers between devices, shift_by(): return lax.ppermute(values, 'freq', [(i, (i + k) % NF) for i in range(NF)])  31.9 us
    ppermute x14, waiting for transfers between devices, shift_by(): return lax.ppermute(values, 'freq', [(i, (i + k) % NF) for i in range(NF)])  29.8 us
    all_to_all x1, starting transfers between devices, on_device(): lax.all_to_all(packed, ('slab', 'freq'), split_axis=0, concat_axis=0, til...  15.7 us
    pallas_call x1, Pallas kernels, on_device(): call(trace_kernel, [sds(NSH, ROWS, cells)] * NF, NF + 7, smem=(0,), scrat...  15.7 us
    pallas_call x1, Pallas kernels, on_device(): call(operator_kernel, [sds(NSH, HALF, CF, dtype=BF)] * 2 + [sds(NSH, CF,...  11.2 us
    pallas_call x1, Pallas kernels, on_device(): call(finish_kernel, [sds(ROWS, NSH * NF, cells)], NF + 3, smem=(0,), scra...  9.88 us
    pallas_call x1, Pallas kernels, on_device(): call(pack_kernel, [sds(SLABS, NF, ROWS, 128), sds(NSH, slots)], 3, scratc...  6.38 us
  transfers between devices with their start and end apart: 15, of which 4 were waited for; matrix products, arithmetic and copies ran while one was open for 6% of the time, Pallas kernels for 14%

profile of v1, /device:TPU:1, one launch (start us, length us, event | category | flops | bytes accessed | tf_op | source)
XLA Modules:
  0.0 236.5 jit_solution(11048956561207473578)
XLA Ops:
  0.0 1.7 copy.15
  1.8 1.7 copy.16.obs_ref
  3.4 6.4 %shard_map.73 = (f32[32,8,24,128]{3,2,1,0:T(8,128)}, f32[4,1024]{1,0:T(4,128)}) custom-call(f32[4,192,512]{2,1,0:T(8,128)} %copy.16.obs_ref, s32[1,1024]{1,0:T(1,128)} %pos_ref.1, s32[4,512]{1,0:T(4,128)} %mute_ref.1), custom_call_target="tpu_custom_call" | custom-call | flops 1610612736 | bytes 4718592 | tf_op jit(solution)/shard_map/pallas_call | solution.py:215
  9.8 15.7 %all-to-all-start = ((f32[256,24,128]{2,1,0:T(8,128)}), f32[256,24,128]{2,1,0:T(8,128)S(1)}, u32[]{:S(2)}, u32[]{:S(2)}) async-start(f32[256,24,128]{2,1,0:T(8,128)} %bitcast.16), calls=%async_computation | async-start | bytes 6291456 | tf_op jit(solution)/shard_map/all_to_all | solution.py:224
  25.5 0.0 copy-start.3
  25.5 0.0 copy-start.4
  25.5 0.0 copy-start.2
  25.5 0.0 copy-start.1
  25.5 4.2 %shard_map.75 = (f32[4,24,1024]{2,1,0:T(8,128)}, f32[4,24,1024]{2,1,0:T(8,128)}, f32[4,24,1024]{2,1,0:T(8,128)}, f32[4,24,1024]{2,1,0:T(8,128)}, f32[4,24,1024]{...) custom-call(s32[1]{0:T(128)} %bitcast.me_ref, f32[24,32,1024]{2,1,0:T(8,128)} %bitcast.17), custom_call_target="tpu_custom_call" | custom-call | bytes 6291456 | tf_op jit(solution)/shard_map/pallas_call | solution.py:228
  29.7 1.6 collective-permute-start
  31.3 1.2 collective-permute-start.1
  32.5 1.7 collective-permute-start.2
  34.2 1.4 collective-permute-start.3
  35.6 2.6 %collective-permute-start.4 = (f32[4,24,1024]{2,1,0:T(8,128)}, f32[4,24,1024]{2,1,0:T(8,128)}, u32[]{:S(2)}, u32[]{:S(2)}) collective-permute-start(f32[4,24,1024]{2,1,0:T(8,128)} %get-tuple-element.37), channel_id=1, source_target_pairs={{0,5},{1,6},{2,7},{3,0},{4,1},{5,2},{6,3},{7,4},{8,13},{9,14},{10,... | collective-permute-start | bytes 1179656 | tf_op jit(solution)/shard_map/ppermute | solution.py:204
  38.2 0.0 copy-done.3
  38.2 0.2 rev.3
  38.4 0.0 copy-done.4
  38.4 0.1 iota_compare_fusion
  38.5 0.6 lt.71
  39.1 0.0 copy-done.2
  39.1 1.0 copy.18
  40.1 0.0 copy-done.1
  40.1 87.1 %all-gather.1 = f32[32,4,1024]{2,1,0:T(4,128)S(1)} all-gather(f32[1,4,1024]{2,1,0:T(4,128)S(1)} %bitcast.19), channel_id=2, replica_groups=mesh['slab'=32,'freq'=8] {'slab'}, dimensions={0}, use_global_device_ids=true | all-gather | bytes 540672 | tf_op jit(solution)/shard_map/all_gather | solution.py:226
  127.2 0.1 dynamic-slice_bitcast_fusion
  127.4 0.1 reshape.142
  127.5 0.6 concatenate.7.taps_ref
  128.1 0.6 concatenate.6.ms_ref
  128.7 1.9 broadcast_select_fusion.cell_ref
  130.6 3.2 %shard_map.74 = (bf16[1024,1024]{1,0:T(8,128)(2,1)}, f32[8,1024]{1,0:T(8,128)}) custom-call(s32[1024,1]{1,0:T(8,128)} %broadcast_select_fusion.cell_ref, f32[8,1024]{1,0:T(8,128)} %concatenate.6.ms_ref), custom_call_target="tpu_custom_call" | custom-call | flops 33554432 | bytes 2097152 | tf_op jit(solution)/shard_map/pallas_call | solution.py:254
  133.8 4.5 %select_multiply_fusion.1.fwd_ref.refs_12_ = f32[192,1024]{1,0:T(8,128)} fusion(s32[192]{0:T(256)S(1)} %fusion.12, pred[192]{0:T(512)(128)(4,1)S(1)} %fusion.16), kind=kLoop, calls=%fused_computation.16 | loop fusion | flops 3342336 | bytes 787392 | tf_op jit(solution)/shard_map/div | solution.py:67
  138.3 5.0 %select_multiply_fusion.inv_ref = f32[1024,192]{1,0:T(8,128)} fusion(s32[192]{0:T(256)S(1)} %fusion.12, pred[192]{0:T(512)(128)(4,1)S(1)} %fusion.16), kind=kLoop, calls=%fused_computation.9 | loop fusion | flops 3342336 | bytes 787392 | tf_op jit(solution)/shard_map/div | solution.py:68
  143.3 0.0 collective-permute-done.refs_1_
  143.3 2.6 %collective-permute-start.5 = (f32[4,24,1024]{2,1,0:T(8,128)}, f32[4,24,1024]{2,1,0:T(8,128)S(1)}, u32[]{:S(2)}, u32[]{:S(2)}) collective-permute-start(f32[4,24,1024]{2,1,0:T(8,128)} %get-tuple-element.38), channel_id=1, source_target_pairs={{0,6},{1,7},{2,0},{3,1},{4,2},{5,3},{6,4},{7,5},{8,14},{9,15},{10,... | collective-permute-start | bytes 1179656 | tf_op jit(solution)/shard_map/ppermute | solution.py:204
  145.9 0.0 collective-permute-done.1.refs_2_
  145.9 0.0 copy-done.5
  145.9 12.2 %collective-permute-start.6 = (f32[4,24,1024]{2,1,0:T(8,128)S(1)}, f32[4,24,1024]{2,1,0:T(8,128)}, u32[]{:S(2)}, u32[]{:S(2)}) collective-permute-start(f32[4,24,1024]{2,1,0:T(8,128)S(1)} %copy-done.5), channel_id=1, source_target_pairs={{0,7},{1,0},{2,1},{3,2},{4,3},{5,4},{6,5},{7,6},{8,15},{9,8},{10,9... | collective-permute-start | bytes 1179656 | tf_op jit(solution)/shard_map/ppermute | solution.py:204
  158.1 11.2 %shard_map.76 = (bf16[4,512,192]{2,1,0:T(8,128)(2,1)}, bf16[4,512,192]{2,1,0:T(8,128)(2,1)}, bf16[4,192,192]{2,1,0:T(8,128)(2,1)}, bf16[4,192,192]{2,1,0:T(8,128)(2,1)}) custom-call(f32[4,512]{1,0:T(4,128)} %concatenate.7.taps_ref, f32[192,1024]{1,0:T(8,128)} %select_multiply_fusion.1.fwd_ref.refs_12_, f32[1024,192]{1,0:T(8,128)} %select_multiply_fusion.inv_ref), custom_call_target="tpu_custom_call" | custom-call | flops 5737807872 | bytes 4194304 | tf_op jit(solution)/shard_map/pallas_call | solution.py:240
  169.3 0.0 collective-permute-done.2.refs_3_
  169.3 0.0 collective-permute-done.3.refs_4_
  169.3 0.0 collective-permute-done.4.refs_5_
  169.3 0.0 collective-permute-done.5.refs_6_
  169.3 0.0 collective-permute-done.6.refs_7_
  169.4 0.7 copy-done.10
  170.1 15.7 %shard_map.77 = (f32[4,24,1024]{2,1,0:T(8,128)}, f32[4,24,1024]{2,1,0:T(8,128)}, f32[4,24,1024]{2,1,0:T(8,128)}, f32[4,24,1024]{2,1,0:T(8,128)}, f32[4,24,1024]{...) custom-call(s32[1]{0:T(128)} %bitcast.me_ref, ...), custom_call_target="tpu_custom_call" | custom-call | flops 5737807872 | bytes 6291456 | tf_op jit(solution)/shard_map/pallas_call | solution.py:262
  185.7 0.0 collective-permute-start.7
  185.7 0.2 collective-permute-start.8
  186.0 2.3 collective-permute-start.9
  188.3 1.2 collective-permute-start.10
  189.5 2.6 %collective-permute-start.11 = (f32[4,24,1024]{2,1,0:T(8,128)}, f32[4,24,1024]{2,1,0:T(8,128)S(1)}, u32[]{:S(2)}, u32[]{:S(2)}) collective-permute-start(f32[4,24,1024]{2,1,0:T(8,128)} %get-tuple-element.50), channel_id=1, source_target_pairs={{0,5},{1,6},{2,7},{3,0},{4,1},{5,2},{6,3},{7,4},{8,13},{9,14},{10,... | collective-permute-start | bytes 1179656 | tf_op jit(solution)/shard_map/ppermute | solution.py:204
  192.1 2.2 collective-permute-done.7.refs_1_
  194.3 2.1 collective-permute-start.12
  196.5 9.8 %collective-permute-done.8.refs_2_ = f32[4,24,1024]{2,1,0:T(8,128)S(1)} collective-permute-done((f32[4,24,1024]{2,1,0:T(8,128)}, f32[4,24,1024]{2,1,0:T(8,128)S(1)}, u32[]{:S(2)}, u32[]{:S(2)}) %collective-permute-start.8) | collective-permute-done | bytes 393248 | tf_op jit(solution)/shard_map/ppermute | solution.py:204
  206.3 0.0 collective-permute-start.13
  206.3 16.8 %collective-permute-done.9.refs_3_ = f32[4,24,1024]{2,1,0:T(8,128)S(1)} collective-permute-done((f32[4,24,1024]{2,1,0:T(8,128)}, f32[4,24,1024]{2,1,0:T(8,128)S(1)}, u32[]{:S(2)}, u32[]{:S(2)}) %collective-permute-start.9) | collective-permute-done | bytes 393248 | tf_op jit(solution)/shard_map/ppermute | solution.py:204
  223.2 0.0 collective-permute-done.10.refs_4_
  223.2 0.0 collective-permute-done.11.refs_5_
  223.2 0.8 collective-permute-done.12.refs_6_
  224.0 0.0 copy-done.9
  224.0 0.2 copy-done.11
  224.2 0.7 copy-done.12
  225.0 0.0 collective-permute-done.13.refs_7_
  225.0 0.0 all-to-all-done
  225.0 1.7 copy-done
  226.6 9.9 %shard_map.78 = f32[24,32,1024]{2,1,0:T(8,128)} custom-call(s32[1]{0:T(128)} %bitcast.me_ref, f32[32,8,24,128]{3,2,1,0:T(8,128)} %bitcast.15, bf16[1024,1024]{1,0:T(8,128)(2,1)} %get-tuple-element.31.hot_ref, f32[4,24,1024]{2,1,0:T(8,128)} %get-tuple-element.45.refs_0_, f32[4,24,1024]{2,1,0:T(8,128)} %copy-done.6, f32[4,24,1024]{2,1,0:T(8,128)} %copy-done.7, ...), custom_call_target="tpu_custom_call" | custom-call | flops 3221225472 | bytes 9437184 | tf_op jit(solution)/shard_map/pallas_call | solution.py:278
  (15 shorter events, 0.1 us)
Async XLA Ops:
  9.8 215.2 %all-to-all-start = ((f32[256,24,128]{2,1,0:T(8,128)}), f32[256,24,128]{2,1,0:T(8,128)S(1)}, u32[]{:S(2)}, u32[]{:S(2)}) async-start(f32[256,24,128]{2,1,0:T(8,128)} %bitcast.16), calls=%async_computation | async-start | bytes 6291456 | tf_op jit(solution)/shard_map/all_to_all | solution.py:224
  25.5 12.7 %copy-start.3 = (f32[4,256]{1,0:T(4,128)S(1)}, f32[4,256]{1,0:T(4,128)}, u32[]{:S(2)}) copy-start(f32[4,256]{1,0:T(4,128)} %param.9) | copy-start | bytes 12292
  25.5 12.9 %copy-start.4 = (s32[1,32]{1,0:T(1,128)S(1)}, s32[1,32]{1,0:T(1,128)}, u32[]{:S(2)}) copy-start(s32[1,32]{1,0:T(1,128)} %param.12) | copy-start | bytes 388
  25.5 13.6 %copy-start.2 = (s32[1,1024]{1,0:T(1,128)S(1)}, s32[1,1024]{1,0:T(1,128)}, u32[]{:S(2)}) copy-start(s32[1,1024]{1,0:T(1,128)} %param.11) | copy-start | bytes 12292
  25.5 14.6 %copy-start.1 = (f32[4,1024]{1,0:T(4,128)S(1)}, f32[4,1024]{1,0:T(4,128)}, u32[]{:S(2)}) copy-start(f32[4,1024]{1,0:T(4,128)} %get-tuple-element.30) | copy-start | bytes 49156
  29.7 113.6 %collective-permute-start = (f32[4,24,1024]{2,1,0:T(8,128)}, f32[4,24,1024]{2,1,0:T(8,128)}, u32[]{:S(2)}, u32[]{:S(2)}) collective-permute-start(f32[4,24,1024]{2,1,0:T(8,128)} %get-tuple-element.33), channel_id=1, source_target_pairs={{0,1},{1,2},{2,3},{3,4},{4,5},{5,6},{6,7},{7,0},{8,9},{9,10},{10,1... | collective-permute-start | bytes 1179656 | tf_op jit(solution)/shard_map/ppermute | solution.py:204
  31.3 114.5 %collective-permute-start.1 = (f32[4,24,1024]{2,1,0:T(8,128)}, f32[4,24,1024]{2,1,0:T(8,128)}, u32[]{:S(2)}, u32[]{:S(2)}) collective-permute-start(f32[4,24,1024]{2,1,0:T(8,128)} %get-tuple-element.34), channel_id=1, source_target_pairs={{0,2},{1,3},{2,4},{3,5},{4,6},{5,7},{6,0},{7,1},{8,10},{9,11},{10,... | collective-permute-start | bytes 1179656 | tf_op jit(solution)/shard_map/ppermute | solution.py:204
  32.5 136.8 %collective-permute-start.2 = (f32[4,24,1024]{2,1,0:T(8,128)}, f32[4,24,1024]{2,1,0:T(8,128)}, u32[]{:S(2)}, u32[]{:S(2)}) collective-permute-start(f32[4,24,1024]{2,1,0:T(8,128)} %get-tuple-element.35), channel_id=1, source_target_pairs={{0,3},{1,4},{2,5},{3,6},{4,7},{5,0},{6,1},{7,2},{8,11},{9,12},{10,... | collective-permute-start | bytes 1179656 | tf_op jit(solution)/shard_map/ppermute | solution.py:204
  34.2 135.1 %collective-permute-start.3 = (f32[4,24,1024]{2,1,0:T(8,128)}, f32[4,24,1024]{2,1,0:T(8,128)}, u32[]{:S(2)}, u32[]{:S(2)}) collective-permute-start(f32[4,24,1024]{2,1,0:T(8,128)} %get-tuple-element.36), channel_id=1, source_target_pairs={{0,4},{1,5},{2,6},{3,7},{4,0},{5,1},{6,2},{7,3},{8,12},{9,13},{10,... | collective-permute-start | bytes 1179656 | tf_op jit(solution)/shard_map/ppermute | solution.py:204
  35.6 133.7 %collective-permute-start.4 = (f32[4,24,1024]{2,1,0:T(8,128)}, f32[4,24,1024]{2,1,0:T(8,128)}, u32[]{:S(2)}, u32[]{:S(2)}) collective-permute-start(f32[4,24,1024]{2,1,0:T(8,128)} %get-tuple-element.37), channel_id=1, source_target_pairs={{0,5},{1,6},{2,7},{3,0},{4,1},{5,2},{6,3},{7,4},{8,13},{9,14},{10,... | collective-permute-start | bytes 1179656 | tf_op jit(solution)/shard_map/ppermute | solution.py:204
  127.5 18.4 %copy-start.5 = (f32[4,24,1024]{2,1,0:T(8,128)S(1)}, f32[4,24,1024]{2,1,0:T(8,128)}, u32[]{:S(2)}) copy-start(f32[4,24,1024]{2,1,0:T(8,128)} %get-tuple-element.39) | copy-start | bytes 1179652
  143.3 26.0 %collective-permute-start.5 = (f32[4,24,1024]{2,1,0:T(8,128)}, f32[4,24,1024]{2,1,0:T(8,128)S(1)}, u32[]{:S(2)}, u32[]{:S(2)}) collective-permute-start(f32[4,24,1024]{2,1,0:T(8,128)} %get-tuple-element.38), channel_id=1, source_target_pairs={{0,6},{1,7},{2,0},{3,1},{4,2},{5,3},{6,4},{7,5},{8,14},{9,15},{10,... | collective-permute-start | bytes 1179656 | tf_op jit(solution)/shard_map/ppermute | solution.py:204
  145.9 23.5 %collective-permute-start.6 = (f32[4,24,1024]{2,1,0:T(8,128)S(1)}, f32[4,24,1024]{2,1,0:T(8,128)}, u32[]{:S(2)}, u32[]{:S(2)}) collective-permute-start(f32[4,24,1024]{2,1,0:T(8,128)S(1)} %copy-done.5), channel_id=1, source_target_pairs={{0,7},{1,0},{2,1},{3,2},{4,3},{5,4},{6,5},{7,6},{8,15},{9,8},{10,9... | collective-permute-start | bytes 1179656 | tf_op jit(solution)/shard_map/ppermute | solution.py:204
  169.3 0.8 copy-start.10
  185.7 8.6 %collective-permute-start.7 = (f32[4,24,1024]{2,1,0:T(8,128)}, f32[4,24,1024]{2,1,0:T(8,128)S(1)}, u32[]{:S(2)}, u32[]{:S(2)}) collective-permute-start(f32[4,24,1024]{2,1,0:T(8,128)} %get-tuple-element.46), channel_id=1, source_target_pairs={{0,1},{1,2},{2,3},{3,4},{4,5},{5,6},{6,7},{7,0},{8,9},{9,10},{10,1... | collective-permute-start | bytes 1179656 | tf_op jit(solution)/shard_map/ppermute | solution.py:204
  185.7 20.6 %collective-permute-start.8 = (f32[4,24,1024]{2,1,0:T(8,128)}, f32[4,24,1024]{2,1,0:T(8,128)S(1)}, u32[]{:S(2)}, u32[]{:S(2)}) collective-permute-start(f32[4,24,1024]{2,1,0:T(8,128)} %get-tuple-element.47), channel_id=1, source_target_pairs={{0,2},{1,3},{2,4},{3,5},{4,6},{5,7},{6,0},{7,1},{8,10},{9,11},{10,... | collective-permute-start | bytes 1179656 | tf_op jit(solution)/shard_map/ppermute | solution.py:204
  186.0 37.2 %collective-permute-start.9 = (f32[4,24,1024]{2,1,0:T(8,128)}, f32[4,24,1024]{2,1,0:T(8,128)S(1)}, u32[]{:S(2)}, u32[]{:S(2)}) collective-permute-start(f32[4,24,1024]{2,1,0:T(8,128)} %get-tuple-element.48), channel_id=1, source_target_pairs={{0,3},{1,4},{2,5},{3,6},{4,7},{5,0},{6,1},{7,2},{8,11},{9,12},{10,... | collective-permute-start | bytes 1179656 | tf_op jit(solution)/shard_map/ppermute | solution.py:204
  188.3 34.9 %collective-permute-start.10 = (f32[4,24,1024]{2,1,0:T(8,128)}, f32[4,24,1024]{2,1,0:T(8,128)S(1)}, u32[]{:S(2)}, u32[]{:S(2)}) collective-permute-start(f32[4,24,1024]{2,1,0:T(8,128)} %get-tuple-element.49), channel_id=1, source_target_pairs={{0,4},{1,5},{2,6},{3,7},{4,0},{5,1},{6,2},{7,3},{8,12},{9,13},{10,... | collective-permute-start | bytes 1179656 | tf_op jit(solution)/shard_map/ppermute | solution.py:204
  189.5 33.7 %collective-permute-start.11 = (f32[4,24,1024]{2,1,0:T(8,128)}, f32[4,24,1024]{2,1,0:T(8,128)S(1)}, u32[]{:S(2)}, u32[]{:S(2)}) collective-permute-start(f32[4,24,1024]{2,1,0:T(8,128)} %get-tuple-element.50), channel_id=1, source_target_pairs={{0,5},{1,6},{2,7},{3,0},{4,1},{5,2},{6,3},{7,4},{8,13},{9,14},{10,... | collective-permute-start | bytes 1179656 | tf_op jit(solution)/shard_map/ppermute | solution.py:204
  194.3 30.6 %copy-start.6 = (f32[4,24,1024]{2,1,0:T(8,128)}, f32[4,24,1024]{2,1,0:T(8,128)S(1)}, u32[]{:S(2)}) copy-start(f32[4,24,1024]{2,1,0:T(8,128)S(1)} %collective-permute-done.7.refs_1_) | copy-start | bytes 1179652
  194.3 29.7 %collective-permute-start.12 = (f32[4,24,1024]{2,1,0:T(8,128)}, f32[4,24,1024]{2,1,0:T(8,128)S(1)}, u32[]{:S(2)}, u32[]{:S(2)}) collective-permute-start(f32[4,24,1024]{2,1,0:T(8,128)} %get-tuple-element.51), channel_id=1, source_target_pairs={{0,6},{1,7},{2,0},{3,1},{4,2},{5,3},{6,4},{7,5},{8,14},{9,15},{10,... | collective-permute-start | bytes 1179656 | tf_op jit(solution)/shard_map/ppermute | solution.py:204
  206.3 17.7 %copy-start.7 = (f32[4,24,1024]{2,1,0:T(8,128)}, f32[4,24,1024]{2,1,0:T(8,128)S(1)}, u32[]{:S(2)}) copy-start(f32[4,24,1024]{2,1,0:T(8,128)S(1)} %collective-permute-done.8.refs_2_) | copy-start | bytes 1179652
  206.3 18.6 %collective-permute-start.13 = (f32[4,24,1024]{2,1,0:T(8,128)}, f32[4,24,1024]{2,1,0:T(8,128)}, u32[]{:S(2)}, u32[]{:S(2)}) collective-permute-start(f32[4,24,1024]{2,1,0:T(8,128)} %get-tuple-element.52), channel_id=1, source_target_pairs={{0,7},{1,0},{2,1},{3,2},{4,3},{5,4},{6,5},{7,6},{8,15},{9,8},{10,9... | collective-permute-start | bytes 1179656 | tf_op jit(solution)/shard_map/ppermute | solution.py:204
  223.2 0.8 copy-start.8
  223.2 0.9 copy-start.9
  223.2 1.0 copy-start.11
  224.2 0.8 copy-start.12
  225.0 1.7 copy-start

commit v2 on v1

--- a/solution.py
+++ b/solution.py
@@ -69,7 +69,7 @@
     return forward, inverse_t
 
 
-def operator_kernel(taps_ref, fwd_ref, inv_ref, gh_ref, gl_ref, bh_ref, bl_ref, g_ref):
+def operator_kernel(taps_ref, fwd_ref, inv_ref, hi_ref, lo_ref, g_ref):
     late = fwd_ref[:, HALF:]
     for n in range(NSH):
         rows = jnp.broadcast_to(taps_ref[n : n + 1, :], (TAPS, 2 * TAPS))
@@ -85,36 +85,52 @@
                 )
             if b < 2:
                 hi, lo = split(g)
-                gh_ref[n, b * TAPS : (b + 1) * TAPS, :] = hi
-                gl_ref[n, b * TAPS : (b + 1) * TAPS, :] = lo
+                hi_ref[n, b * TAPS : (b + 1) * TAPS, :] = hi
+                lo_ref[n, b * TAPS : (b + 1) * TAPS, :] = lo
             else:
                 g_ref[(b - 2) * TAPS : (b - 1) * TAPS, :] = g
         hi, lo = split(jnp.dot(late, g_ref[...], precision=lax.Precision.HIGHEST))
-        bh_ref[n] = hi
-        bl_ref[n] = lo
-
-
-def pack_kernel(obs_ref, pos_ref, mute_ref, out_ref, ms_ref, y_ref):
-    group = obs_ref.shape[2]
+        hi_ref[n, HALF:, :] = hi
+        lo_ref[n, HALF:, :] = lo
+
+
+def mute_kernel(pos_ref, mute_ref, ms_ref):
+    group = mute_ref.shape[1]
     slots = pos_ref.shape[1]
     pick = (
         lax.broadcasted_iota(jnp.int32, (group, slots), 0) == jnp.broadcast_to(pos_ref[...], (group, slots))
     ).astype(F32).astype(BF)
     mh, ml = split(mute_ref[...].astype(F32))
     ms_ref[...] = mm(mh, pick) + mm(ml, pick)
-    for n in range(NSH):
-        hi, lo = split(obs_ref[n])
-        y_ref[n] = mm(hi, pick) + mm(lo, pick)
-    lane = lax.broadcasted_iota(jnp.int32, (CF, 128), 1) // SLOT
+
+
+def pack_kernel(me_ref, pos_ref, *refs):
+    blocks = refs[:NF]
+    out_ref, x_ref, y_ref = refs[NF:]
+    me = me_ref[0]
+    group = x_ref.shape[2]
+    slots = pos_ref.shape[1]
+    part = CF
+    for k in range(NF):
+        x_ref[:, k * NSH : (k + 1) * NSH, :] = blocks[k][...]
+    pick = (
+        lax.broadcasted_iota(jnp.int32, (group, slots), 0) == jnp.broadcast_to(pos_ref[...], (group, slots))
+    ).astype(F32).astype(BF)
+    each = ROWS // 4
+    for g in range(4):
+        x = pltpu.roll(x_ref[g * each : (g + 1) * each], me * NSH, 1)
+        hi, lo = split(x.reshape(part, group))
+        y_ref[g] = mm(hi, pick) + mm(lo, pick)
+    lane = lax.broadcasted_iota(jnp.int32, (part, 128), 1) // SLOT
     for tile in range(SLABS // 4):
-        parts = [y_ref[n, :, tile * 128 : (tile + 1) * 128] for n in range(NSH)]
+        parts = [y_ref[g, :, tile * 128 : (tile + 1) * 128] for g in range(4)]
         for b in range(4):
             acc = None
-            for n in range(NSH):
-                shift = ((n - b) % 4) * SLOT
-                v = pltpu.roll(parts[n], shift, 1) if shift else parts[n]
-                acc = v if acc is None else jnp.where(lane == n, v, acc)
-            out_ref[4 * tile + b] = acc.reshape(NF, ROWS, 128)
+            for g in range(4):
+                shift = ((g - b) % 4) * SLOT
+                v = pltpu.roll(parts[g], shift, 1) if shift else parts[g]
+                acc = v if acc is None else jnp.where(lane == g, v, acc)
+            out_ref[4 * tile + b] = acc
 
 
 def route_kernel(me_ref, x_ref, *refs):
@@ -140,13 +156,13 @@
 
 def trace_kernel(me_ref, *refs):
     xs = refs[:NF]
-    gh_ref, gl_ref, bh_ref, bl_ref, fwd_ref, mc_ref = refs[NF : NF + 6]
-    outs = refs[NF + 6 : 2 * NF + 6]
-    fh_ref, fl_ref, x_ref, r_ref = refs[2 * NF + 6 :]
+    hi_ref, lo_ref, fwd_ref, mc_ref = refs[NF : NF + 4]
+    outs = refs[NF + 4 : 2 * NF + 4]
+    f_ref, x_ref, r_ref = refs[2 * NF + 4 :]
     me = me_ref[0]
     fh, fl = split(fwd_ref[:, :HALF])
-    fh_ref[...] = fh
-    fl_ref[...] = fl
+    f_ref[:CF] = fh
+    f_ref[CF:] = fl
     cells = x_ref.shape[1]
     width = 256
     t = lax.broadcasted_iota(jnp.int32, (HALF, width), 0).astype(F32)
@@ -161,14 +177,16 @@
             live = mc_ref[NSH : NSH + 1, at]
             x = jnp.where(live > 0.5, x_ref[:, at], 0.0)
             xh, xl = split(x)
-            gh = gh_ref[n]
-            y = mm(gh, xh) + mm(gh, xl) + mm(gl_ref[n], xh)
+            table = hi_ref[n]
+            u = mm(table, xh)
+            v = mm(lo_ref[n], xh)
+            z = mm(table, xl)
             cut = mc_ref[pl.ds(n, 1), at]
-            y = jnp.where(t >= cut, y, 0.0)
+            y = jnp.where(t >= cut, u[:HALF] + v[:HALF] + z[:HALF], 0.0)
+            r = u[HALF:] + v[HALF:] + z[HALF:]
             yh, yl = split(y)
-            bh = bh_ref[n]
-            r = mm(fh_ref[...], yh) + mm(fh_ref[...], yl) + mm(fl_ref[...], yh)
-            r = r + mm(bh, xh) + mm(bh, xl) + mm(bl_ref[n], xh)
+            p = mm(f_ref[...], yh)
+            r = r + p[:CF] + p[CF:] + mm(f_ref[:CF], yl)
             r_ref[:, at] = r
         for k in range(NF):
             j = lax.rem(me + k, NF)
@@ -178,26 +196,29 @@
 def finish_kernel(me_ref, z_ref, hot_ref, *refs):
     rs = refs[:NF]
     out_ref = refs[NF]
-    a_ref, p_ref, s_ref = refs[NF + 1 :]
+    a_ref, s_ref = refs[NF + 1 :]
     me = me_ref[0]
-    lane = lax.broadcasted_iota(jnp.int32, (NF, ROWS, 128), 2) // SLOT
-    for n in range(NSH):
+    for k in range(NF):
+        j = lax.rem(me - k + NF, NF)
+        s_ref[pl.ds(j * NSH, NSH)] = rs[k][...]
+    for o in range(4):
+        out_ref[:, 8 * o : 8 * o + 8, :] = jnp.swapaxes(s_ref[8 * o : 8 * o + 8], 0, 1)
+    lane = lax.broadcasted_iota(jnp.int32, (CF, 128), 1) // SLOT
+    each = ROWS // 4
+    for g in range(4):
         for tile in range(SLABS // 4):
             acc = None
             for e in range(4):
-                shift = ((e - n) % 4) * SLOT
+                shift = ((e - g) % 4) * SLOT
                 v = z_ref[4 * tile + e]
                 if shift:
-                    v = pltpu.roll(v, shift, 2)
+                    v = pltpu.roll(v, shift, 1)
                 acc = v if acc is None else jnp.where(lane == e, v, acc)
-            a_ref[:, tile * 128 : (tile + 1) * 128] = acc.reshape(CF, 128)
+            a_ref[:, tile * 128 : (tile + 1) * 128] = acc
         hi, lo = split(a_ref[...])
-        p_ref[...] = mm(hi, hot_ref[...]) + mm(lo, hot_ref[...])
-        for k in range(NF):
-            j = lax.rem(me - k + NF, NF)
-            s_ref[j * NSH + n] = rs[k][n] - p_ref[pl.ds(pl.multiple_of(j * ROWS, 8), ROWS), :]
-    for o in range(4):
-        out_ref[:, 8 * o : 8 * o + 8, :] = jnp.swapaxes(s_ref[8 * o : 8 * o + 8], 0, 1)
+        p = mm(hi, hot_ref[...]) + mm(lo, hot_ref[...])
+        at = slice(g * each, (g + 1) * each)
+        out_ref[at] = out_ref[at] - p.reshape(each, NSH * NF, p.shape[1])
 
 
 def shift_by(values, k):
@@ -208,22 +229,31 @@
     cells = wavefield.shape[3]
     group = observed.shape[3]
     slots = send_cell.shape[1]
-    slab = lax.axis_index("slab")
     me = lax.axis_index("freq").astype(jnp.int32).reshape(1)
 
-    obs = observed.reshape(2, NF, FB, NSH, group).transpose(3, 1, 0, 2, 4).reshape(NSH, CF, group)
-    packed, mute_slots = call(
+    (mute_slots,) = call(mute_kernel, [sds(NSH, slots)], 2, flops=1 << 26, nbytes=1 << 16)(
+        recv_pos, mute
+    )
+    mute_slots = mute_slots.reshape(NSH, SLABS, SLOT).transpose(1, 0, 2).reshape(SLABS, 1, 128)
+    mine = lax.all_to_all(mute_slots, "slab", split_axis=0, concat_axis=0, tiled=True)
+    obs = observed.reshape(2, NF, FB, NSH, group)
+    own = [
+        lax.dynamic_index_in_dim(obs, lax.rem(me[0] + NF - k, NF), 1, keepdims=False).reshape(
+            ROWS, NSH, group
+        )
+        for k in range(NF)
+    ]
+    own = [own[0]] + [shift_by(own[k], NF - k) for k in range(1, NF)]
+    (packed,) = call(
         pack_kernel,
-        [sds(SLABS, NF, ROWS, 128), sds(NSH, slots)],
-        3,
-        scratch=[pltpu.VMEM((NSH, CF, slots), F32)],
+        [sds(SLABS, CF, 128)],
+        NF + 2,
+        smem=(0,),
+        scratch=[pltpu.VMEM((ROWS, NSH * NF, group), F32), pltpu.VMEM((4, CF, slots), F32)],
         flops=2 * 2 * NSH * CF * group * slots,
         nbytes=4 * NSH * CF * (group + slots),
-    )(obs, recv_pos, mute)
-    packed = packed.reshape(SLABS * NF, ROWS, 128)
-    arrived = lax.all_to_all(packed, ("slab", "freq"), split_axis=0, concat_axis=0, tiled=True)
-    arrived = arrived.reshape(SLABS, NF, ROWS, 128)
-    mute_all = lax.all_gather(mute_slots, "slab")
+    )(me, recv_pos, *own)
+    arrived = lax.all_to_all(packed, "slab", split_axis=0, concat_axis=0, tiled=True)
 
     blocks = call(
         route_kernel,
@@ -237,9 +267,9 @@
 
     forward, inverse_t = tables()
     taps = jnp.concatenate([filters[:, ::-1], jnp.zeros_like(filters)], axis=1)
-    gh, gl, bh, bl = call(
+    hi, lo = call(
         operator_kernel,
-        [sds(NSH, HALF, CF, dtype=BF)] * 2 + [sds(NSH, CF, CF, dtype=BF)] * 2,
+        [sds(NSH, HALF + CF, CF, dtype=BF)] * 2,
         3,
         scratch=[pltpu.VMEM((HALF, CF), F32)],
         flops=6 * 2 * NSH * CF * (1024 * 512 + CF * HALF),
@@ -248,8 +278,7 @@
 
     live = jnp.arange(SLOT, dtype=jnp.int32)[None, :] < send_count[0][:, None]
     target = jnp.where(live.reshape(-1), send_cell[0], -1).reshape(slots, 1)
-    mine = lax.dynamic_slice(mute_all, (0, 0, slab * SLOT), (SLABS, NSH, SLOT))
-    mine = mine.transpose(1, 0, 2).reshape(NSH, slots)
+    mine = mine.reshape(SLABS, NSH, SLOT).transpose(1, 0, 2).reshape(NSH, slots)
     mine = jnp.concatenate([mine, jnp.ones((NSH, slots), F32)], axis=0)
     hot, at_cells = call(
         place_kernel,
@@ -262,17 +291,16 @@
     results = call(
         trace_kernel,
         [sds(NSH, ROWS, cells)] * NF,
-        NF + 7,
+        NF + 5,
         smem=(0,),
         scratch=[
-            pltpu.VMEM((CF, HALF), BF),
-            pltpu.VMEM((CF, HALF), BF),
+            pltpu.VMEM((2 * CF, HALF), BF),
             pltpu.VMEM((CF, cells), F32),
             pltpu.VMEM((CF, cells), F32),
         ],
         flops=6 * NSH * cells * (2 * CF * HALF + CF * CF),
         nbytes=8 * NSH * CF * cells,
-    )(me, *spectra, gh, gl, bh, bl, forward, at_cells)
+    )(me, *spectra, hi, lo, forward, at_cells)
     returned = [results[0]] + [shift_by(results[k], k) for k in range(1, NF)]
 
     (out,) = call(
@@ -282,7 +310,6 @@
         smem=(0,),
         scratch=[
             pltpu.VMEM((CF, slots), F32),
-            pltpu.VMEM((CF, cells), F32),
             pltpu.VMEM((NSH * NF, ROWS, cells), F32),
         ],
         flops=4 * NSH * CF * slots * cells,

time: 238 us -> 159 us (0.67)
  blocking collectives: 87.1 us -> 0 us
  waiting for transfers between devices: 29.8 us -> 40 us
    all_gather x1 -> x0, blocking collectives: 87.1 us -> none  [on_device(): mute_all = lax.all_gather(mute_slots, 'slab')]
    ppermute x14 -> x21, waiting for transfers between devices: 29.8 us -> 38.8 us  [shift_by(): return lax.ppermute(values, 'freq', [(i, (i + k) % NF) for i in range(NF)])]
    ppermute x14 -> x21, starting transfers between devices: 31.9 us -> 25.9 us  [shift_by(): return lax.ppermute(values, 'freq', [(i, (i + k) % NF) for i in range(NF)])]
    all_to_all x1 -> x2, starting transfers between devices: 15.7 us -> 19.3 us  [the longest x1 11.3 us: on_device(): lax.all_to_all(mute_slots, 'slab', split_axis=0, concat_axis=0, tiled=True)]
    dynamic_slice x0 -> x1, local copies, waits for them, and re-layouts: none -> 2.45 us  [on_device(): lax.dynamic_index_in_dim(obs, lax.rem(me[0] + NF - k, NF), 1, keepdims=Fa...]
    pallas_call x3 -> x4, Pallas kernels: 33.2 us -> 32.9 us  [the longest x1 12.7 us: on_device(): call(trace_kernel, [sds(NSH, ROWS, cells)] * NF, NF + 5, smem=(0,), scrat...]
  transfers between devices with their start and end apart: 15 -> 23, of which waited for: 4 -> 7; matrix products, arithmetic and copies ran while one was open for 6% -> 11% of each run, Pallas kernels for 14% -> 25%
where the time goes in v2:
time: 159 us; the launch traced here: 158 us
  Pallas kernels  49.8 us (31%)
  starting transfers between devices  45.2 us (28%)
  waiting for transfers between devices  40 us (25%)
  other arithmetic  12.1 us (8%)
  local copies, waits for them, and re-layouts  11 us (7%)
    ppermute x21, waiting for transfers between devices, shift_by(): return lax.ppermute(values, 'freq', [(i, (i + k) % NF) for i in range(NF)])  38.8 us
    ppermute x21, starting transfers between devices, shift_by(): return lax.ppermute(values, 'freq', [(i, (i + k) % NF) for i in range(NF)])  25.9 us
    pallas_call x1, Pallas kernels, on_device(): call(trace_kernel, [sds(NSH, ROWS, cells)] * NF, NF + 5, smem=(0,), scrat...  12.7 us
    pallas_call x1, Pallas kernels, on_device(): call(operator_kernel, [sds(NSH, HALF + CF, CF, dtype=BF)] * 2, 3, scratch...  12 us
    all_to_all x1, starting transfers between devices, on_device(): lax.all_to_all(mute_slots, 'slab', split_axis=0, concat_axis=0, tiled=True)  11.3 us
    pallas_call x1, Pallas kernels, on_device(): call(finish_kernel, [sds(ROWS, NSH * NF, cells)], NF + 3, smem=(0,), scra...  9.48 us
    all_to_all x1, starting transfers between devices, on_device(): lax.all_to_all(packed, 'slab', split_axis=0, concat_axis=0, tiled=True)  8.05 us
    pallas_call x1, Pallas kernels, on_device(): call(pack_kernel, [sds(SLABS, CF, 128)], NF + 2, smem=(0,), scratch=[pltp...  6.42 us
  transfers between devices with their start and end apart: 23, of which 7 were waited for; matrix products, arithmetic and copies ran while one was open for 11% of the time, Pallas kernels for 25%

profile of v2, /device:TPU:1, one launch (start us, length us, event | category | flops | bytes accessed | tf_op | source)
XLA Modules:
  0.0 158.3 jit_solution(14655068769060897025)
XLA Ops:
  0.0 2.4 %constant_dynamic-slice_fusion = (f32[2,1,12,4,512]{4,3,2,1,0:T(4,128)S(1)}, f32[2,1,12,4,512]{4,3,2,1,0:T(4,128)S(1)}, f32[2,1,12,4,512]{4,3,2,1,0:T(4,128)S(1)...) fusion(f32[2,8,12,4,512]{4,3,2,1,0:T(4,128)} %bitcast.36, ...), kind=kLoop, calls=%fused_computation.26 | loop fusion | bytes 3145760 | tf_op jit(solution)/shard_map/jit(dynamic_index_in_dim)/dynamic_slice | solution.py:241
  2.4 2.1 %collective-permute-start.5 = (f32[24,4,512]{2,1,0:T(4,128)S(1)}, f32[24,4,512]{2,1,0:T(4,128)S(1)}, u32[]{:S(2)}, u32[]{:S(2)}) collective-permute-start(f32[24,4,512]{2,1,0:T(4,128)S(1)} %bitcast.46), channel_id=1, source_target_pairs={{0,2},{1,3},{2,4},{3,5},{4,6},{5,7},{6,0},{7,1},{8,10},{9,11},{10,... | collective-permute-start | bytes 589832 | tf_op jit(solution)/shard_map/ppermute | solution.py:225
  4.6 2.1 %collective-permute-start.6 = (f32[24,4,512]{2,1,0:T(4,128)S(1)}, f32[24,4,512]{2,1,0:T(4,128)S(1)}, u32[]{:S(2)}, u32[]{:S(2)}) collective-permute-start(f32[24,4,512]{2,1,0:T(4,128)S(1)} %bitcast.45), channel_id=1, source_target_pairs={{0,1},{1,2},{2,3},{3,4},{4,5},{5,6},{6,7},{7,0},{8,9},{9,10},{10,1... | collective-permute-start | bytes 589832 | tf_op jit(solution)/shard_map/ppermute | solution.py:225
  6.7 1.3 collective-permute-start.4
  8.0 1.7 %collective-permute-start.3 = (f32[24,4,512]{2,1,0:T(4,128)S(1)}, f32[24,4,512]{2,1,0:T(4,128)S(1)}, u32[]{:S(2)}, u32[]{:S(2)}) collective-permute-start(f32[24,4,512]{2,1,0:T(4,128)S(1)} %bitcast.43), channel_id=1, source_target_pairs={{0,4},{1,5},{2,6},{3,7},{4,0},{5,1},{6,2},{7,3},{8,12},{9,13},{10,... | collective-permute-start | bytes 589832 | tf_op jit(solution)/shard_map/ppermute | solution.py:225
  9.7 2.6 %collective-permute-start.2 = (f32[24,4,512]{2,1,0:T(4,128)S(1)}, f32[24,4,512]{2,1,0:T(4,128)S(1)}, u32[]{:S(2)}, u32[]{:S(2)}) collective-permute-start(f32[24,4,512]{2,1,0:T(4,128)S(1)} %bitcast.42), channel_id=1, source_target_pairs={{0,5},{1,6},{2,7},{3,0},{4,1},{5,2},{6,3},{7,4},{8,13},{9,14},{10,... | collective-permute-start | bytes 589832 | tf_op jit(solution)/shard_map/ppermute | solution.py:225
  12.4 0.0 collective-permute-done.6.refs_7_
  12.4 2.4 %collective-permute-start = (f32[24,4,512]{2,1,0:T(4,128)S(1)}, f32[24,4,512]{2,1,0:T(4,128)S(1)}, u32[]{:S(2)}, u32[]{:S(2)}) collective-permute-start(f32[24,4,512]{2,1,0:T(4,128)S(1)} %bitcast.40), channel_id=1, source_target_pairs={{0,7},{1,0},{2,1},{3,2},{4,3},{5,4},{6,5},{7,6},{8,15},{9,8},{10,9... | collective-permute-start | bytes 589832 | tf_op jit(solution)/shard_map/ppermute | solution.py:225
  14.8 1.8 %shard_map.74 = f32[4,1024]{1,0:T(4,128)} custom-call(s32[1,1024]{1,0:T(1,128)} %pos_ref.3, s32[4,512]{1,0:T(4,128)} %mute_ref.1), custom_call_target="tpu_custom_call" | custom-call | flops 67108864 | bytes 65536 | tf_op jit(solution)/shard_map/pallas_call | solution.py:234
  16.6 0.8 reshape.179
  17.4 0.7 reshape.180
  18.1 11.3 %all-to-all-start.1 = ((f32[32,1,128]{2,1,0:T(1,128)}), f32[32,1,128]{2,1,0:T(1,128)S(1)}, u32[]{:S(2)}, u32[]{:S(2)}) async-start(f32[32,1,128]{2,1,0:T(1,128)} %bitcast.13), calls=%async_computation.1 | async-start | bytes 32768 | tf_op jit(solution)/shard_map/all_to_all | solution.py:238
  29.4 0.0 collective-permute-done.4.refs_5_
  29.4 0.0 collective-permute-done.3.refs_4_
  29.5 0.0 collective-permute-done.1.refs_2_
  29.5 0.0 collective-permute-done.refs_1_
  29.5 0.6 copy-done.12
  30.1 0.1 copy-done.13
  30.2 0.1 copy-done.14
  30.2 0.1 copy-done.15
  30.3 0.1 copy-done.16
  30.4 6.4 %shard_map.73 = f32[32,192,128]{2,1,0:T(8,128)} custom-call(s32[1]{0:T(128)} %bitcast.me_ref, s32[1,1024]{1,0:T(1,128)} %pos_ref.3, f32[24,4,512]{2,1,0:T(4,128)} %bitcast.39, f32[24,4,512]{2,1,0:T(4,128)} %copy-done.16, f32[24,4,512]{2,1,0:T(4,128)} %copy-done.15, f32[24,4,512]{2,1,0:T(4,128)} %copy-done.14, f32[24,4,512]{2,1,0:T(4,128)} %copy-done.13, ...), custom_call_target="tpu_custom_call" | custom-call | flops 1610612736 | bytes 4718592 | tf_op jit(solution)/shard_map/pallas_call | solution.py:247
  36.8 1.2 all-to-all-done.1
  38.0 8.1 %all-to-all-start = ((f32[32,192,128]{2,1,0:T(8,128)}), f32[32,192,128]{2,1,0:T(8,128)S(1)}, u32[]{:S(2)}, u32[]{:S(2)}) async-start(f32[32,192,128]{2,1,0:T(8,128)} %shard_map.73), calls=%async_computation | async-start | bytes 6291456 | tf_op jit(solution)/shard_map/all_to_all | solution.py:256
  46.1 0.0 copy-start.2
  46.1 4.2 %shard_map.76 = (f32[4,24,1024]{2,1,0:T(8,128)}, f32[4,24,1024]{2,1,0:T(8,128)}, f32[4,24,1024]{2,1,0:T(8,128)}, f32[4,24,1024]{2,1,0:T(8,128)}, f32[4,24,1024]{...) custom-call(s32[1]{0:T(128)} %bitcast.me_ref, f32[24,32,1024]{2,1,0:T(8,128)} %bitcast.35), custom_call_target="tpu_custom_call" | custom-call | bytes 6291456 | tf_op jit(solution)/shard_map/pallas_call | solution.py:258
  50.3 0.7 collective-permute-start.7
  51.0 1.4 collective-permute-start.8
  52.4 1.5 collective-permute-start.9
  54.0 1.0 collective-permute-start.10
  54.9 2.6 %collective-permute-start.11 = (f32[4,24,1024]{2,1,0:T(8,128)}, f32[4,24,1024]{2,1,0:T(8,128)}, u32[]{:S(2)}, u32[]{:S(2)}) collective-permute-start(f32[4,24,1024]{2,1,0:T(8,128)} %get-tuple-element.31), channel_id=1, source_target_pairs={{0,5},{1,6},{2,7},{3,0},{4,1},{5,2},{6,3},{7,4},{8,13},{9,14},{10,... | collective-permute-start | bytes 1179656 | tf_op jit(solution)/shard_map/ppermute | solution.py:225
  57.6 0.2 rev.3
  57.7 0.6 concatenate.7.taps_ref
  58.4 4.5 %select_multiply_fusion.1.fwd_ref.refs_10_ = f32[192,1024]{1,0:T(8,128)} fusion(s32[192]{0:T(256)S(1)} %fusion.12, pred[192]{0:T(512)(128)(4,1)S(1)} %fusion.16), kind=kLoop, calls=%fused_computation.16 | loop fusion | flops 3342336 | bytes 787392 | tf_op jit(solution)/shard_map/div | solution.py:67
  62.8 5.0 %select_multiply_fusion.inv_ref = f32[1024,192]{1,0:T(8,128)} fusion(s32[192]{0:T(256)S(1)} %fusion.12, pred[192]{0:T(512)(128)(4,1)S(1)} %fusion.16), kind=kLoop, calls=%fused_computation.9 | loop fusion | flops 3342336 | bytes 787392 | tf_op jit(solution)/shard_map/div | solution.py:68
  67.9 12.0 %shard_map.77 = (bf16[4,704,192]{2,1,0:T(8,128)(2,1)}, bf16[4,704,192]{2,1,0:T(8,128)(2,1)}) custom-call(f32[4,512]{1,0:T(4,128)} %concatenate.7.taps_ref, f32[192,1024]{1,0:T(8,128)} %select_multiply_fusion.1.fwd_ref.refs_10_, f32[1024,192]{1,0:T(8,128)} %select_multiply_fusion.inv_ref), custom_call_target="tpu_custom_call" | custom-call | flops 5737807872 | bytes 4194304 | tf_op jit(solution)/shard_map/pallas_call | solution.py:270
  79.8 0.0 collective-permute-done.7.refs_1_
  79.8 0.0 collective-permute-start.12
  79.8 1.2 collective-permute-start.13
  81.1 0.1 iota_compare_fusion
  81.1 0.6 lt.100
  81.7 1.0 copy.37
  82.7 1.9 %broadcast_select_fusion.cell_ref = s32[1024,1]{1,0:T(8,128)} fusion(pred[1024,1]{1,0:T(8,128)(4,1)S(1)} %lt.100, s32[1024,1]{1,0:T(8,128)} %copy.37), kind=kLoop, calls=%fused_computation.20 | loop fusion | flops 1024 | bytes 9216 | tf_op jit(solution)/shard_map/jit(_where)/select_n | solution.py:280
  84.6 0.5 broadcast.218
  85.1 0.6 reduce.3
  85.7 0.1 reshape.181
  85.8 0.1 reshape.182
  85.9 0.6 concatenate.6.ms_ref
  86.5 3.2 %shard_map.75 = (bf16[1024,1024]{1,0:T(8,128)(2,1)}, f32[8,1024]{1,0:T(8,128)}) custom-call(s32[1024,1]{1,0:T(8,128)} %broadcast_select_fusion.cell_ref, f32[8,1024]{1,0:T(8,128)} %concatenate.6.ms_ref), custom_call_target="tpu_custom_call" | custom-call | flops 33554432 | bytes 2097152 | tf_op jit(solution)/shard_map/pallas_call | solution.py:283
  89.7 0.0 collective-permute-done.9.refs_3_
  89.7 1.3 collective-permute-done.12.refs_6_
  91.0 4.3 %collective-permute-done.13.refs_7_ = f32[4,24,1024]{2,1,0:T(8,128)} collective-permute-done((f32[4,24,1024]{2,1,0:T(8,128)}, f32[4,24,1024]{2,1,0:T(8,128)}, u32[]{:S(2)}, u32[]{:S(2)}) %collective-permute-start.13) | collective-permute-done | bytes 393248 | tf_op jit(solution)/shard_map/ppermute | solution.py:225
  95.4 12.7 %shard_map.78 = (f32[4,24,1024]{2,1,0:T(8,128)}, f32[4,24,1024]{2,1,0:T(8,128)}, f32[4,24,1024]{2,1,0:T(8,128)}, f32[4,24,1024]{2,1,0:T(8,128)}, f32[4,24,1024]{...) custom-call(s32[1]{0:T(128)} %bitcast.me_ref, ...), custom_call_target="tpu_custom_call" | custom-call | flops 5737807872 | bytes 6291456 | tf_op jit(solution)/shard_map/pallas_call | solution.py:291
  108.1 0.1 collective-permute-start.15
  108.2 3.0 %collective-permute-start.16 = (f32[4,24,1024]{2,1,0:T(8,128)}, f32[4,24,1024]{2,1,0:T(8,128)S(1)}, u32[]{:S(2)}, u32[]{:S(2)}) collective-permute-start(f32[4,24,1024]{2,1,0:T(8,128)} %get-tuple-element.40), channel_id=1, source_target_pairs={{0,3},{1,4},{2,5},{3,6},{4,7},{5,0},{6,1},{7,2},{8,11},{9,12},{10,... | collective-permute-start | bytes 1179656 | tf_op jit(solution)/shard_map/ppermute | solution.py:225
  111.2 0.3 collective-permute-start.17
  111.5 1.8 %collective-permute-start.18 = (f32[4,24,1024]{2,1,0:T(8,128)}, f32[4,24,1024]{2,1,0:T(8,128)S(1)}, u32[]{:S(2)}, u32[]{:S(2)}) collective-permute-start(f32[4,24,1024]{2,1,0:T(8,128)} %get-tuple-element.42), channel_id=1, source_target_pairs={{0,5},{1,6},{2,7},{3,0},{4,1},{5,2},{6,3},{7,4},{8,13},{9,14},{10,... | collective-permute-start | bytes 1179656 | tf_op jit(solution)/shard_map/ppermute | solution.py:225
  113.2 3.5 %collective-permute-done.14.refs_1_ = f32[4,24,1024]{2,1,0:T(8,128)S(1)} collective-permute-done((f32[4,24,1024]{2,1,0:T(8,128)}, f32[4,24,1024]{2,1,0:T(8,128)S(1)}, u32[]{:S(2)}, u32[]{:S(2)}) %collective-permute-start.14) | collective-permute-done | bytes 393248 | tf_op jit(solution)/shard_map/ppermute | solution.py:225
  116.7 9.6 %collective-permute-done.15.refs_2_ = f32[4,24,1024]{2,1,0:T(8,128)S(1)} collective-permute-done((f32[4,24,1024]{2,1,0:T(8,128)}, f32[4,24,1024]{2,1,0:T(8,128)S(1)}, u32[]{:S(2)}, u32[]{:S(2)}) %collective-permute-start.15) | collective-permute-done | bytes 393248 | tf_op jit(solution)/shard_map/ppermute | solution.py:225
  126.4 17.8 %collective-permute-done.16.refs_3_ = f32[4,24,1024]{2,1,0:T(8,128)S(1)} collective-permute-done((f32[4,24,1024]{2,1,0:T(8,128)}, f32[4,24,1024]{2,1,0:T(8,128)S(1)}, u32[]{:S(2)}, u32[]{:S(2)}) %collective-permute-start.16) | collective-permute-done | bytes 393248 | tf_op jit(solution)/shard_map/ppermute | solution.py:225
  144.2 2.2 %collective-permute-done.19.refs_6_ = f32[4,24,1024]{2,1,0:T(8,128)S(1)} collective-permute-done((f32[4,24,1024]{2,1,0:T(8,128)}, f32[4,24,1024]{2,1,0:T(8,128)S(1)}, u32[]{:S(2)}, u32[]{:S(2)}) %collective-permute-start.19) | collective-permute-done | bytes 393248 | tf_op jit(solution)/shard_map/ppermute | solution.py:225
  146.4 0.7 copy-done.9
  147.2 1.7 %copy-done = f32[32,192,128]{2,1,0:T(8,128)} copy-done((f32[32,192,128]{2,1,0:T(8,128)}, f32[32,192,128]{2,1,0:T(8,128)S(1)}, u32[]{:S(2)}) %copy-start) | copy-done | bytes 3145752
  148.8 9.5 %shard_map.79 = f32[24,32,1024]{2,1,0:T(8,128)} custom-call(s32[1]{0:T(128)} %bitcast.me_ref, f32[32,192,128]{2,1,0:T(8,128)} %copy-done, bf16[1024,1024]{1,0:T(8,128)(2,1)} %get-tuple-element.25.hot_ref, f32[4,24,1024]{2,1,0:T(8,128)} %get-tuple-element.37.refs_0_, f32[4,24,1024]{2,1,0:T(8,128)} %copy-done.4, f32[4,24,1024]{2,1,0:T(8,128)} %copy-done.5, ...), custom_call_target="tpu_custom_call" | custom-call | flops 3221225472 | bytes 9437184 | tf_op jit(solution)/shard_map/pallas_call | solution.py:306
  (43 shorter events, 0.2 us)
Async XLA Ops:
  2.4 9.9 %collective-permute-start.5 = (f32[24,4,512]{2,1,0:T(4,128)S(1)}, f32[24,4,512]{2,1,0:T(4,128)S(1)}, u32[]{:S(2)}, u32[]{:S(2)}) collective-permute-start(f32[24,4,512]{2,1,0:T(4,128)S(1)} %bitcast.46), channel_id=1, source_target_pairs={{0,2},{1,3},{2,4},{3,5},{4,6},{5,7},{6,0},{7,1},{8,10},{9,11},{10,... | collective-permute-start | bytes 589832 | tf_op jit(solution)/shard_map/ppermute | solution.py:225
  4.6 7.8 %collective-permute-start.6 = (f32[24,4,512]{2,1,0:T(4,128)S(1)}, f32[24,4,512]{2,1,0:T(4,128)S(1)}, u32[]{:S(2)}, u32[]{:S(2)}) collective-permute-start(f32[24,4,512]{2,1,0:T(4,128)S(1)} %bitcast.45), channel_id=1, source_target_pairs={{0,1},{1,2},{2,3},{3,4},{4,5},{5,6},{6,7},{7,0},{8,9},{9,10},{10,1... | collective-permute-start | bytes 589832 | tf_op jit(solution)/shard_map/ppermute | solution.py:225
  6.7 22.7 %collective-permute-start.4 = (f32[24,4,512]{2,1,0:T(4,128)S(1)}, f32[24,4,512]{2,1,0:T(4,128)S(1)}, u32[]{:S(2)}, u32[]{:S(2)}) collective-permute-start(f32[24,4,512]{2,1,0:T(4,128)S(1)} %bitcast.44), channel_id=1, source_target_pairs={{0,3},{1,4},{2,5},{3,6},{4,7},{5,0},{6,1},{7,2},{8,11},{9,12},{10,... | collective-permute-start | bytes 589832 | tf_op jit(solution)/shard_map/ppermute | solution.py:225
  8.0 21.4 %collective-permute-start.3 = (f32[24,4,512]{2,1,0:T(4,128)S(1)}, f32[24,4,512]{2,1,0:T(4,128)S(1)}, u32[]{:S(2)}, u32[]{:S(2)}) collective-permute-start(f32[24,4,512]{2,1,0:T(4,128)S(1)} %bitcast.43), channel_id=1, source_target_pairs={{0,4},{1,5},{2,6},{3,7},{4,0},{5,1},{6,2},{7,3},{8,12},{9,13},{10,... | collective-permute-start | bytes 589832 | tf_op jit(solution)/shard_map/ppermute | solution.py:225
  9.7 19.7 %collective-permute-start.2 = (f32[24,4,512]{2,1,0:T(4,128)S(1)}, f32[24,4,512]{2,1,0:T(4,128)S(1)}, u32[]{:S(2)}, u32[]{:S(2)}) collective-permute-start(f32[24,4,512]{2,1,0:T(4,128)S(1)} %bitcast.42), channel_id=1, source_target_pairs={{0,5},{1,6},{2,7},{3,0},{4,1},{5,2},{6,3},{7,4},{8,13},{9,14},{10,... | collective-permute-start | bytes 589832 | tf_op jit(solution)/shard_map/ppermute | solution.py:225
  12.3 17.2 %copy-start.10 = (f32[24,4,512]{2,1,0:T(4,128)}, f32[24,4,512]{2,1,0:T(4,128)S(1)}, u32[]{:S(2)}) copy-start(f32[24,4,512]{2,1,0:T(4,128)S(1)} %collective-permute-done.5.refs_6_) | copy-start | bytes 589828
  12.3 17.1 %collective-permute-start.1 = (f32[24,4,512]{2,1,0:T(4,128)S(1)}, f32[24,4,512]{2,1,0:T(4,128)S(1)}, u32[]{:S(2)}, u32[]{:S(2)}) collective-permute-start(f32[24,4,512]{2,1,0:T(4,128)S(1)} %bitcast.41), channel_id=1, source_target_pairs={{0,6},{1,7},{2,0},{3,1},{4,2},{5,3},{6,4},{7,5},{8,14},{9,15},{10,... | collective-permute-start | bytes 589832 | tf_op jit(solution)/shard_map/ppermute | solution.py:225
  12.4 17.2 %copy-start.11 = (f32[24,4,512]{2,1,0:T(4,128)}, f32[24,4,512]{2,1,0:T(4,128)S(1)}, u32[]{:S(2)}) copy-start(f32[24,4,512]{2,1,0:T(4,128)S(1)} %collective-permute-done.6.refs_7_) | copy-start | bytes 589828
  12.4 17.1 %collective-permute-start = (f32[24,4,512]{2,1,0:T(4,128)S(1)}, f32[24,4,512]{2,1,0:T(4,128)S(1)}, u32[]{:S(2)}, u32[]{:S(2)}) collective-permute-start(f32[24,4,512]{2,1,0:T(4,128)S(1)} %bitcast.40), channel_id=1, source_target_pairs={{0,7},{1,0},{2,1},{3,2},{4,3},{5,4},{6,5},{7,6},{8,15},{9,8},{10,9... | collective-permute-start | bytes 589832 | tf_op jit(solution)/shard_map/ppermute | solution.py:225
  18.1 19.9 %all-to-all-start.1 = ((f32[32,1,128]{2,1,0:T(1,128)}), f32[32,1,128]{2,1,0:T(1,128)S(1)}, u32[]{:S(2)}, u32[]{:S(2)}) async-start(f32[32,1,128]{2,1,0:T(1,128)} %bitcast.13), calls=%async_computation.1 | async-start | bytes 32768 | tf_op jit(solution)/shard_map/all_to_all | solution.py:238
  29.4 0.7 copy-start.12
  29.4 0.7 copy-start.13
  29.5 0.8 copy-start.14
  29.5 0.8 copy-start.15
  29.5 0.9 copy-start.16
  38.0 109.2 %all-to-all-start = ((f32[32,192,128]{2,1,0:T(8,128)}), f32[32,192,128]{2,1,0:T(8,128)S(1)}, u32[]{:S(2)}, u32[]{:S(2)}) async-start(f32[32,192,128]{2,1,0:T(8,128)} %shard_map.73), calls=%async_computation | async-start | bytes 6291456 | tf_op jit(solution)/shard_map/all_to_all | solution.py:256
  46.1 11.5 %copy-start.2 = (f32[4,256]{1,0:T(4,128)S(1)}, f32[4,256]{1,0:T(4,128)}, u32[]{:S(2)}) copy-start(f32[4,256]{1,0:T(4,128)} %param.9) | copy-start | bytes 12292
  50.3 29.5 %collective-permute-start.7 = (f32[4,24,1024]{2,1,0:T(8,128)}, f32[4,24,1024]{2,1,0:T(8,128)}, u32[]{:S(2)}, u32[]{:S(2)}) collective-permute-start(f32[4,24,1024]{2,1,0:T(8,128)} %get-tuple-element.27), channel_id=1, source_target_pairs={{0,1},{1,2},{2,3},{3,4},{4,5},{5,6},{6,7},{7,0},{8,9},{9,10},{10,1... | collective-permute-start | bytes 1179656 | tf_op jit(solution)/shard_map/ppermute | solution.py:225
  51.0 28.8 %collective-permute-start.8 = (f32[4,24,1024]{2,1,0:T(8,128)}, f32[4,24,1024]{2,1,0:T(8,128)}, u32[]{:S(2)}, u32[]{:S(2)}) collective-permute-start(f32[4,24,1024]{2,1,0:T(8,128)} %get-tuple-element.28), channel_id=1, source_target_pairs={{0,2},{1,3},{2,4},{3,5},{4,6},{5,7},{6,0},{7,1},{8,10},{9,11},{10,... | collective-permute-start | bytes 1179656 | tf_op jit(solution)/shard_map/ppermute | solution.py:225
  52.4 37.3 %collective-permute-start.9 = (f32[4,24,1024]{2,1,0:T(8,128)}, f32[4,24,1024]{2,1,0:T(8,128)}, u32[]{:S(2)}, u32[]{:S(2)}) collective-permute-start(f32[4,24,1024]{2,1,0:T(8,128)} %get-tuple-element.29), channel_id=1, source_target_pairs={{0,3},{1,4},{2,5},{3,6},{4,7},{5,0},{6,1},{7,2},{8,11},{9,12},{10,... | collective-permute-start | bytes 1179656 | tf_op jit(solution)/shard_map/ppermute | solution.py:225
  54.0 35.8 %collective-permute-start.10 = (f32[4,24,1024]{2,1,0:T(8,128)}, f32[4,24,1024]{2,1,0:T(8,128)}, u32[]{:S(2)}, u32[]{:S(2)}) collective-permute-start(f32[4,24,1024]{2,1,0:T(8,128)} %get-tuple-element.30), channel_id=1, source_target_pairs={{0,4},{1,5},{2,6},{3,7},{4,0},{5,1},{6,2},{7,3},{8,12},{9,13},{10,... | collective-permute-start | bytes 1179656 | tf_op jit(solution)/shard_map/ppermute | solution.py:225
  54.9 34.8 %collective-permute-start.11 = (f32[4,24,1024]{2,1,0:T(8,128)}, f32[4,24,1024]{2,1,0:T(8,128)}, u32[]{:S(2)}, u32[]{:S(2)}) collective-permute-start(f32[4,24,1024]{2,1,0:T(8,128)} %get-tuple-element.31), channel_id=1, source_target_pairs={{0,5},{1,6},{2,7},{3,0},{4,1},{5,2},{6,3},{7,4},{8,13},{9,14},{10,... | collective-permute-start | bytes 1179656 | tf_op jit(solution)/shard_map/ppermute | solution.py:225
  67.9 13.2 %copy-start.3 = (s32[1,32]{1,0:T(1,128)S(1)}, s32[1,32]{1,0:T(1,128)}, u32[]{:S(2)}) copy-start(s32[1,32]{1,0:T(1,128)} %param.12) | copy-start | bytes 388
  67.9 13.9 %copy-start.1 = (s32[1,1024]{1,0:T(1,128)S(1)}, s32[1,1024]{1,0:T(1,128)}, u32[]{:S(2)}) copy-start(s32[1,1024]{1,0:T(1,128)} %param.11) | copy-start | bytes 12292
  79.8 11.2 %collective-permute-start.12 = (f32[4,24,1024]{2,1,0:T(8,128)}, f32[4,24,1024]{2,1,0:T(8,128)}, u32[]{:S(2)}, u32[]{:S(2)}) collective-permute-start(f32[4,24,1024]{2,1,0:T(8,128)} %get-tuple-element.32), channel_id=1, source_target_pairs={{0,6},{1,7},{2,0},{3,1},{4,2},{5,3},{6,4},{7,5},{8,14},{9,15},{10,... | collective-permute-start | bytes 1179656 | tf_op jit(solution)/shard_map/ppermute | solution.py:225
  79.8 15.5 %collective-permute-start.13 = (f32[4,24,1024]{2,1,0:T(8,128)}, f32[4,24,1024]{2,1,0:T(8,128)}, u32[]{:S(2)}, u32[]{:S(2)}) collective-permute-start(f32[4,24,1024]{2,1,0:T(8,128)} %get-tuple-element.33), channel_id=1, source_target_pairs={{0,7},{1,0},{2,1},{3,2},{4,3},{5,4},{6,5},{7,6},{8,15},{9,8},{10,9... | collective-permute-start | bytes 1179656 | tf_op jit(solution)/shard_map/ppermute | solution.py:225
  108.1 8.6 %collective-permute-start.14 = (f32[4,24,1024]{2,1,0:T(8,128)}, f32[4,24,1024]{2,1,0:T(8,128)S(1)}, u32[]{:S(2)}, u32[]{:S(2)}) collective-permute-start(f32[4,24,1024]{2,1,0:T(8,128)} %get-tuple-element.38), channel_id=1, source_target_pairs={{0,1},{1,2},{2,3},{3,4},{4,5},{5,6},{6,7},{7,0},{8,9},{9,10},{10,1... | collective-permute-start | bytes 1179656 | tf_op jit(solution)/shard_map/ppermute | solution.py:225
  108.1 18.2 %collective-permute-start.15 = (f32[4,24,1024]{2,1,0:T(8,128)}, f32[4,24,1024]{2,1,0:T(8,128)S(1)}, u32[]{:S(2)}, u32[]{:S(2)}) collective-permute-start(f32[4,24,1024]{2,1,0:T(8,128)} %get-tuple-element.39), channel_id=1, source_target_pairs={{0,2},{1,3},{2,4},{3,5},{4,6},{5,7},{6,0},{7,1},{8,10},{9,11},{10,... | collective-permute-start | bytes 1179656 | tf_op jit(solution)/shard_map/ppermute | solution.py:225
  108.2 36.0 %collective-permute-start.16 = (f32[4,24,1024]{2,1,0:T(8,128)}, f32[4,24,1024]{2,1,0:T(8,128)S(1)}, u32[]{:S(2)}, u32[]{:S(2)}) collective-permute-start(f32[4,24,1024]{2,1,0:T(8,128)} %get-tuple-element.40), channel_id=1, source_target_pairs={{0,3},{1,4},{2,5},{3,6},{4,7},{5,0},{6,1},{7,2},{8,11},{9,12},{10,... | collective-permute-start | bytes 1179656 | tf_op jit(solution)/shard_map/ppermute | solution.py:225
  111.2 33.0 %collective-permute-start.17 = (f32[4,24,1024]{2,1,0:T(8,128)}, f32[4,24,1024]{2,1,0:T(8,128)S(1)}, u32[]{:S(2)}, u32[]{:S(2)}) collective-permute-start(f32[4,24,1024]{2,1,0:T(8,128)} %get-tuple-element.41), channel_id=1, source_target_pairs={{0,4},{1,5},{2,6},{3,7},{4,0},{5,1},{6,2},{7,3},{8,12},{9,13},{10,... | collective-permute-start | bytes 1179656 | tf_op jit(solution)/shard_map/ppermute | solution.py:225
  111.5 32.7 %collective-permute-start.18 = (f32[4,24,1024]{2,1,0:T(8,128)}, f32[4,24,1024]{2,1,0:T(8,128)S(1)}, u32[]{:S(2)}, u32[]{:S(2)}) collective-permute-start(f32[4,24,1024]{2,1,0:T(8,128)} %get-tuple-element.42), channel_id=1, source_target_pairs={{0,5},{1,6},{2,7},{3,0},{4,1},{5,2},{6,3},{7,4},{8,13},{9,14},{10,... | collective-permute-start | bytes 1179656 | tf_op jit(solution)/shard_map/ppermute | solution.py:225
  116.7 30.5 %copy-start.4 = (f32[4,24,1024]{2,1,0:T(8,128)}, f32[4,24,1024]{2,1,0:T(8,128)S(1)}, u32[]{:S(2)}) copy-start(f32[4,24,1024]{2,1,0:T(8,128)S(1)} %collective-permute-done.14.refs_1_) | copy-start | bytes 1179652
  116.7 29.7 %collective-permute-start.19 = (f32[4,24,1024]{2,1,0:T(8,128)}, f32[4,24,1024]{2,1,0:T(8,128)S(1)}, u32[]{:S(2)}, u32[]{:S(2)}) collective-permute-start(f32[4,24,1024]{2,1,0:T(8,128)} %get-tuple-element.43), channel_id=1, source_target_pairs={{0,6},{1,7},{2,0},{3,1},{4,2},{5,3},{6,4},{7,5},{8,14},{9,15},{10,... | collective-permute-start | bytes 1179656 | tf_op jit(solution)/shard_map/ppermute | solution.py:225
  126.3 20.1 %copy-start.5 = (f32[4,24,1024]{2,1,0:T(8,128)}, f32[4,24,1024]{2,1,0:T(8,128)S(1)}, u32[]{:S(2)}) copy-start(f32[4,24,1024]{2,1,0:T(8,128)S(1)} %collective-permute-done.15.refs_2_) | copy-start | bytes 1179652
  126.4 20.8 %collective-permute-start.20 = (f32[4,24,1024]{2,1,0:T(8,128)}, f32[4,24,1024]{2,1,0:T(8,128)}, u32[]{:S(2)}, u32[]{:S(2)}) collective-permute-start(f32[4,24,1024]{2,1,0:T(8,128)} %get-tuple-element.44), channel_id=1, source_target_pairs={{0,7},{1,0},{2,1},{3,2},{4,3},{5,4},{6,5},{7,6},{8,15},{9,8},{10,9... | collective-permute-start | bytes 1179656 | tf_op jit(solution)/shard_map/ppermute | solution.py:225
  144.2 2.2 %copy-start.6 = (f32[4,24,1024]{2,1,0:T(8,128)}, f32[4,24,1024]{2,1,0:T(8,128)S(1)}, u32[]{:S(2)}) copy-start(f32[4,24,1024]{2,1,0:T(8,128)S(1)} %collective-permute-done.16.refs_3_) | copy-start | bytes 1179652
  144.2 2.2 %copy-start.7 = (f32[4,24,1024]{2,1,0:T(8,128)}, f32[4,24,1024]{2,1,0:T(8,128)S(1)}, u32[]{:S(2)}) copy-start(f32[4,24,1024]{2,1,0:T(8,128)S(1)} %collective-permute-done.17.refs_4_) | copy-start | bytes 1179652
  144.2 2.2 %copy-start.8 = (f32[4,24,1024]{2,1,0:T(8,128)}, f32[4,24,1024]{2,1,0:T(8,128)S(1)}, u32[]{:S(2)}) copy-start(f32[4,24,1024]{2,1,0:T(8,128)S(1)} %collective-permute-done.18.refs_5_) | copy-start | bytes 1179652
  146.4 0.7 copy-start.9
  147.2 1.7 %copy-start = (f32[32,192,128]{2,1,0:T(8,128)}, f32[32,192,128]{2,1,0:T(8,128)S(1)}, u32[]{:S(2)}) copy-start(f32[32,192,128]{2,1,0:T(8,128)S(1)} %all-to-all-done.z_ref) | copy-start | bytes 9437188
